TPU v7x, 32 devices: a whole 2x2x4 slice. The times are simulated.
32 devices in a mesh: rep: 4 (over y, x), shard: 8 (over z, core).
Axes of the slice: x: 2, y: 2, z: 4, core: 2. Of those that a mesh axis runs over, the one named last changes fastest.
Arguments:
- hidden: bfloat16 [32768, 768], P(('rep', 'shard')), may hold values from -6 to 6
- segment_ids: int32 [32, 1024], P(('rep', 'shard')), may hold values from 0 to 7, never falling along the last dimension, each value on 1 to 800 neighbouring positions
- cotangent: bfloat16 [32768, 768], P(('rep', 'shard'))
- w_query: bfloat16 [768, 384], P('shard'), may hold values from -0.21875 to 0.21875
- w_key: bfloat16 [768, 384], P('shard'), may hold values from -0.21875 to 0.21875
- w_value: bfloat16 [768, 384], P('shard'), may hold values from -0.21875 to 0.21875
- w_depth: bfloat16 [9, 768], P(None, 'shard'), may hold values from -2 to 2
- w_keyconv: bfloat16 [768, 384], P('shard'), may hold values from -0.21875 to 0.21875
- w_kernel: bfloat16 [54, 384], P(None, 'shard'), may hold values from -0.3125 to 0.3125
- w_convout: bfloat16 [768, 384], P('shard'), may hold values from -0.21875 to 0.21875
- w_output: bfloat16 [768, 768], P('shard'), may hold values from -0.875 to 0.875
- gain_attn: bfloat16 [768], P('shard'), may hold values from 0.5 to 1.5
- w_inter: bfloat16 [2, 384, 1536], P(None, None, 'shard'), may hold values from -0.3125 to 0.3125
- w_outer: bfloat16 [2, 1536, 384], P(None, 'shard'), may hold values from -0.15625 to 0.15625
- gain_ffn: bfloat16 [768], P('shard'), may hold values from 0.5 to 1.5
Outputs:
- output: bfloat16 [32768, 768], P(('rep', 'shard'))
- hidden_grad: float32 [32768, 768], P(('rep', 'shard'))
- grad_query: float32 [768, 384], P('shard')
- grad_key: float32 [768, 384], P('shard')
- grad_value: float32 [768, 384], P('shard')
- grad_depth: float32 [9, 768], P(None, 'shard')
- grad_keyconv: float32 [768, 384], P('shard')
- grad_kernel: float32 [54, 384], P(None, 'shard')
- grad_convout: float32 [768, 384], P('shard')
- grad_output: float32 [768, 768], P('shard')
- grad_gain_attn: float32 [768], P('shard')
- grad_inter: float32 [2, 384, 1536], P(None, None, 'shard')
- grad_outer: float32 [2, 1536, 384], P(None, 'shard')
- grad_gain_ffn: float32 [768], P('shard')
Inputs may be any that keep to these rules, and one draw needn't show every extreme that they name: `segment_ids`: segment ids never fall along a sequence; each of the 8 documents of a sequence has 1 to 800 tokens, one exactly 800.
All inputs are finite; a program needn't handle non-finite values.
Results may differ from a plain program's by a relative error of at most 0.015.
Values may be sent and summed in bfloat16 or wider, within the bound.
A program may use at most 192 MiB of HBM per device.

v0:
```python
import jax
import jax.numpy as jnp
from jax import lax
from jax.sharding import PartitionSpec as P

epsilon = 1e-05
masked_value = -1000000000.0
inv_root_two = 0.7071067811865476


def product(left, right):
    return jnp.dot(left, right, preferred_element_type=jnp.float32)


def product_t(left, right):
    return lax.dot_general(
        left, right, (((0,), (0,)), ((), ())), preferred_element_type=jnp.float32
    )


def product_nt(left, right):
    return lax.dot_general(
        left, right, (((1,), (1,)), ((), ())), preferred_element_type=jnp.float32
    )


def shifted(value, segment, offset, half_taps):
    length = value.shape[1]
    padded = jnp.pad(value, ((0, 0), (half_taps, half_taps), (0, 0)))
    seg_padded = jnp.pad(segment, ((0, 0), (half_taps, half_taps)), constant_values=-1)
    moved_rows = lax.slice_in_dim(padded, half_taps + offset, half_taps + offset + length, axis=1)
    moved_segs = lax.slice_in_dim(
        seg_padded, half_taps + offset, half_taps + offset + length, axis=1
    )
    same_doc = moved_segs == segment
    return jnp.where(same_doc[:, :, None], moved_rows, jnp.zeros_like(moved_rows))


def normalize(value, gain_row):
    centered = value - jnp.mean(value, axis=1, keepdims=True)
    row_scale = lax.rsqrt(jnp.mean(centered * centered, axis=1, keepdims=True) + epsilon)
    unit_rows = centered * row_scale
    return (unit_rows * gain_row[None, :], unit_rows, row_scale)


def normalize_back(grad_rows, unit_rows, row_scale, gain_row):
    gain_grad = jnp.sum(grad_rows * unit_rows, axis=0)
    scaled = grad_rows * gain_row[None, :]
    inside = (
        scaled
        - jnp.mean(scaled, axis=1, keepdims=True)
        - unit_rows * jnp.mean(scaled * unit_rows, axis=1, keepdims=True)
    )
    return (row_scale * inside, gain_grad)


def gelu_exact(value):
    return 0.5 * value * (1.0 + lax.erf(value * inv_root_two))


def block_scores(query_block, keys_seq, seg_block, seg_seq):
    head_scale = query_block.shape[2] ** (-0.5)
    raw_scores = (
        jnp.einsum("qhd,khd->hqk", query_block, keys_seq, preferred_element_type=jnp.float32)
        * head_scale
    )
    live = (seg_block[:, None] == seg_seq[None, :])[None, :, :]
    return jnp.where(live, raw_scores, masked_value)


def attend_forward(seq_item):
    queries_seq, keys_seq, values_seq, seg_seq = seq_item
    length, heads, head_size = queries_seq.shape
    block = min(512, length)
    count = length // block

    def one_block(block_item):
        query_block, seg_block = block_item
        scores = block_scores(query_block, keys_seq, seg_block, seg_seq)
        row_top = jnp.max(scores, axis=2, keepdims=True)
        weights = jnp.exp(scores - row_top)
        totals = jnp.sum(weights, axis=2, keepdims=True)
        probs_low = (weights / totals).astype(jnp.bfloat16)
        attended = jnp.einsum(
            "hqk,khd->qhd", probs_low, values_seq, preferred_element_type=jnp.float32
        )
        return (attended, (row_top + jnp.log(totals))[:, :, 0])

    attended, lse_blocks = lax.map(
        one_block,
        (queries_seq.reshape(count, block, heads, head_size), seg_seq.reshape(count, block)),
    )
    return (attended.reshape(length, heads, head_size), lse_blocks)


def attend_back(seq_item):
    queries_seq, keys_seq, values_seq, seg_seq, lse_blocks, grad_seq = seq_item
    length, heads, head_size = queries_seq.shape
    block = min(512, length)
    count = length // block
    head_scale = head_size ** (-0.5)

    def one_block(carry, block_item):
        keys_acc, values_acc = carry
        query_block, seg_block, lse_block, grad_block = block_item
        scores = block_scores(query_block, keys_seq, seg_block, seg_seq)
        probs = jnp.exp(scores - lse_block[:, :, None])
        values_acc = values_acc + jnp.einsum(
            "hqk,qhd->khd",
            probs.astype(jnp.bfloat16),
            grad_block,
            preferred_element_type=jnp.float32,
        )
        grad_probs = jnp.einsum(
            "qhd,khd->hqk", grad_block, values_seq, preferred_element_type=jnp.float32
        )
        grad_scores = (
            probs * (grad_probs - jnp.sum(grad_probs * probs, axis=2, keepdims=True))
        ).astype(jnp.bfloat16)
        query_grad = (
            jnp.einsum("hqk,khd->qhd", grad_scores, keys_seq, preferred_element_type=jnp.float32)
            * head_scale
        )
        keys_acc = (
            keys_acc
            + jnp.einsum(
                "hqk,qhd->khd", grad_scores, query_block, preferred_element_type=jnp.float32
            )
            * head_scale
        )
        return ((keys_acc, values_acc), query_grad)

    zero_heads = jnp.zeros((length, heads, head_size), jnp.float32)
    block_items = (
        queries_seq.reshape(count, block, heads, head_size),
        seg_seq.reshape(count, block),
        lse_blocks,
        grad_seq.reshape(count, block, heads, head_size),
    )
    (keys_acc, values_acc), query_grads = lax.scan(one_block, (zero_heads, zero_heads), block_items)
    return (query_grads.reshape(length, heads, head_size), keys_acc, values_acc)


def layer_forward(seq_rows, segment, params):
    (
        w_query,
        w_key,
        w_value,
        w_depth,
        w_keyconv,
        w_kernel,
        w_convout,
        w_output,
        gain_attn,
        w_inter,
        w_outer,
        gain_ffn,
    ) = params
    seqs, length, model = seq_rows.shape
    taps_count = w_depth.shape[0]
    half_taps = (taps_count - 1) // 2
    att_width = w_query.shape[1]
    heads = w_kernel.shape[0] // taps_count
    head_size = att_width // heads
    groups = w_inter.shape[0]
    tokens = seqs * length
    flat_rows = seq_rows.reshape(tokens, model)
    queries = product(flat_rows, w_query).astype(jnp.bfloat16)
    keys_low = product(flat_rows, w_key).astype(jnp.bfloat16)
    values_low = product(flat_rows, w_value).astype(jnp.bfloat16)
    depth_sum = jnp.zeros((seqs, length, model), jnp.float32)
    for tap_index in range(taps_count):
        depth_sum = depth_sum + w_depth[tap_index].astype(jnp.float32) * shifted(
            seq_rows, segment, tap_index - half_taps, half_taps
        ).astype(jnp.float32)
    depth_low = depth_sum.reshape(tokens, model).astype(jnp.bfloat16)
    keyconv = product(depth_low, w_keyconv)
    mixed_key = (keyconv * queries.astype(jnp.float32)).astype(jnp.bfloat16)
    logits = product_nt(mixed_key, w_kernel).reshape(seqs, length, heads, taps_count)
    row_top = jnp.max(logits, axis=3, keepdims=True)
    weights = jnp.exp(logits - row_top)
    tap_weights = weights / jnp.sum(weights, axis=3, keepdims=True)
    conv_values = product(flat_rows, w_convout).reshape(seqs, length, att_width)
    conv_mix = jnp.zeros((seqs, length, heads, head_size), jnp.float32)
    for tap_index in range(taps_count):
        moved = shifted(conv_values, segment, tap_index - half_taps, half_taps).reshape(
            seqs, length, heads, head_size
        )
        conv_mix = conv_mix + tap_weights[:, :, :, tap_index, None] * moved
    head_shape = (seqs, length, heads, head_size)
    attended, lse_blocks = lax.map(
        attend_forward,
        (
            queries.reshape(head_shape),
            keys_low.reshape(head_shape),
            values_low.reshape(head_shape),
            segment,
        ),
    )
    context = jnp.concatenate(
        [attended.reshape(tokens, att_width), conv_mix.reshape(tokens, att_width)], axis=1
    ).astype(jnp.bfloat16)
    first_sum = product(context, w_output) + flat_rows.astype(jnp.float32)
    normed, unit_one, scale_one = normalize(first_sum, gain_attn.astype(jnp.float32))
    normed_low = normed.astype(jnp.bfloat16).reshape(tokens, groups, model // groups)
    inner = jnp.einsum("ngd,gdf->ngf", normed_low, w_inter, preferred_element_type=jnp.float32)
    activated = gelu_exact(inner).astype(jnp.bfloat16)
    second_sum = (
        jnp.einsum("ngf,gfd->ngd", activated, w_outer, preferred_element_type=jnp.float32).reshape(
            tokens, model
        )
        + normed
    )
    result, unit_two, scale_two = normalize(second_sum, gain_ffn.astype(jnp.float32))
    return {
        "flat_rows": flat_rows,
        "queries": queries,
        "keys_low": keys_low,
        "values_low": values_low,
        "depth_low": depth_low,
        "keyconv": keyconv,
        "mixed_key": mixed_key,
        "tap_weights": tap_weights,
        "conv_values": conv_values,
        "lse_blocks": lse_blocks,
        "context": context,
        "unit_one": unit_one,
        "scale_one": scale_one,
        "normed_low": normed_low,
        "inner": inner,
        "activated": activated,
        "unit_two": unit_two,
        "scale_two": scale_two,
        "result": result,
    }


def layer_backward(seq_rows, segment, params, saved, grad_rows):
    (
        w_query,
        w_key,
        w_value,
        w_depth,
        w_keyconv,
        w_kernel,
        w_convout,
        w_output,
        gain_attn,
        w_inter,
        w_outer,
        gain_ffn,
    ) = params
    seqs, length, model = seq_rows.shape
    taps_count = w_depth.shape[0]
    half_taps = (taps_count - 1) // 2
    att_width = w_query.shape[1]
    heads = w_kernel.shape[0] // taps_count
    head_size = att_width // heads
    groups = w_inter.shape[0]
    tokens = seqs * length
    flat_rows = saved["flat_rows"]
    grad_top = grad_rows.astype(jnp.float32)
    d_second, grad_gain_ffn = normalize_back(
        grad_top, saved["unit_two"], saved["scale_two"], gain_ffn.astype(jnp.float32)
    )
    d_branch = d_second.astype(jnp.bfloat16).reshape(tokens, groups, model // groups)
    grad_outer = jnp.einsum(
        "ngf,ngd->gfd", saved["activated"], d_branch, preferred_element_type=jnp.float32
    )
    d_activated = jnp.einsum("ngd,gfd->ngf", d_branch, w_outer, preferred_element_type=jnp.float32)
    unused, gelu_pull = jax.vjp(gelu_exact, saved["inner"])
    d_inner = gelu_pull(d_activated)[0].astype(jnp.bfloat16)
    grad_inter = jnp.einsum(
        "ngd,ngf->gdf", saved["normed_low"], d_inner, preferred_element_type=jnp.float32
    )
    d_normed = d_second + jnp.einsum(
        "ngf,gdf->ngd", d_inner, w_inter, preferred_element_type=jnp.float32
    ).reshape(tokens, model)
    d_first, grad_gain_attn = normalize_back(
        d_normed, saved["unit_one"], saved["scale_one"], gain_attn.astype(jnp.float32)
    )
    d_out = d_first.astype(jnp.bfloat16)
    grad_output = product_t(saved["context"], d_out)
    d_context = product_nt(d_out, w_output).astype(jnp.bfloat16)
    d_attended = d_context[:, :att_width]
    d_conv = d_context[:, att_width:].astype(jnp.float32).reshape(seqs, length, heads, head_size)
    tap_weights = saved["tap_weights"]
    conv_values = saved["conv_values"]
    d_conv_values = jnp.zeros((seqs, length, att_width), jnp.float32)
    tap_grads = []
    for tap_index in range(taps_count):
        offset = tap_index - half_taps
        moved = shifted(conv_values, segment, offset, half_taps).reshape(
            seqs, length, heads, head_size
        )
        tap_grads.append(jnp.sum(d_conv * moved, axis=3))
        spread_back = (tap_weights[:, :, :, tap_index, None] * d_conv).reshape(
            seqs, length, att_width
        )
        d_conv_values = d_conv_values + shifted(spread_back, segment, -offset, half_taps)
    d_taps = jnp.stack(tap_grads, axis=3)
    d_logits = (
        (tap_weights * (d_taps - jnp.sum(d_taps * tap_weights, axis=3, keepdims=True)))
        .astype(jnp.bfloat16)
        .reshape(tokens, heads * taps_count)
    )
    grad_kernel = product_t(d_logits, saved["mixed_key"])
    d_mixed = product(d_logits, w_kernel).astype(jnp.bfloat16).astype(jnp.float32)
    queries = saved["queries"]
    d_keyconv = (d_mixed * queries.astype(jnp.float32)).astype(jnp.bfloat16)
    grad_keyconv = product_t(saved["depth_low"], d_keyconv)
    d_depth = (
        product_nt(d_keyconv, w_keyconv)
        .astype(jnp.bfloat16)
        .astype(jnp.float32)
        .reshape(seqs, length, model)
    )
    depth_rows = []
    depth_back = jnp.zeros((seqs, length, model), jnp.float32)
    for tap_index in range(taps_count):
        offset = tap_index - half_taps
        moved = shifted(seq_rows, segment, offset, half_taps).astype(jnp.float32)
        depth_rows.append(jnp.sum(d_depth * moved, axis=(0, 1)))
        depth_back = depth_back + shifted(
            d_depth * w_depth[tap_index].astype(jnp.float32), segment, -offset, half_taps
        )
    grad_depth = jnp.stack(depth_rows, axis=0)
    d_values_conv = d_conv_values.reshape(tokens, att_width).astype(jnp.bfloat16)
    grad_convout = product_t(flat_rows, d_values_conv)
    head_shape = (seqs, length, heads, head_size)
    attn_items = (
        queries.reshape(head_shape),
        saved["keys_low"].reshape(head_shape),
        saved["values_low"].reshape(head_shape),
        segment,
        saved["lse_blocks"],
        d_attended.reshape(head_shape),
    )
    query_part, keys_part, values_part = lax.map(attend_back, attn_items)
    d_queries = (query_part.reshape(tokens, att_width) + d_mixed * saved["keyconv"]).astype(
        jnp.bfloat16
    )
    d_keys = keys_part.reshape(tokens, att_width).astype(jnp.bfloat16)
    d_values = values_part.reshape(tokens, att_width).astype(jnp.bfloat16)
    grad_query = product_t(flat_rows, d_queries)
    grad_key = product_t(flat_rows, d_keys)
    grad_value = product_t(flat_rows, d_values)
    hidden_grad = (
        d_first
        + product_nt(d_queries, w_query)
        + product_nt(d_keys, w_key)
        + product_nt(d_values, w_value)
        + product_nt(d_values_conv, w_convout)
        + depth_back.reshape(tokens, model)
    )
    gradients = (
        grad_query,
        grad_key,
        grad_value,
        grad_depth,
        grad_keyconv,
        grad_kernel,
        grad_convout,
        grad_output,
        grad_gain_attn,
        grad_inter,
        grad_outer,
        grad_gain_ffn,
    )
    return (hidden_grad, gradients)


def local(
    hidden,
    segment_ids,
    cotangent,
    w_query,
    w_key,
    w_value,
    w_depth,
    w_keyconv,
    w_kernel,
    w_convout,
    w_output,
    gain_attn,
    w_inter,
    w_outer,
    gain_ffn,
):
    seqs = segment_ids.shape[0]
    length = segment_ids.shape[1]
    seq_rows = hidden.reshape(seqs, length, hidden.shape[1])
    params = (
        lax.all_gather(w_query, "shard", axis=0, tiled=True),
        lax.all_gather(w_key, "shard", axis=0, tiled=True),
        lax.all_gather(w_value, "shard", axis=0, tiled=True),
        lax.all_gather(w_depth, "shard", axis=1, tiled=True),
        lax.all_gather(w_keyconv, "shard", axis=0, tiled=True),
        lax.all_gather(w_kernel, "shard", axis=1, tiled=True),
        lax.all_gather(w_convout, "shard", axis=0, tiled=True),
        lax.all_gather(w_output, "shard", axis=0, tiled=True),
        lax.all_gather(gain_attn, "shard", axis=0, tiled=True),
        lax.all_gather(w_inter, "shard", axis=2, tiled=True),
        lax.all_gather(w_outer, "shard", axis=1, tiled=True),
        lax.all_gather(gain_ffn, "shard", axis=0, tiled=True),
    )
    first_pass = layer_forward(seq_rows, segment_ids, params)
    output = first_pass["result"].astype(jnp.bfloat16)
    params_back = (
        lax.all_gather(w_query, "shard", axis=0, tiled=True),
        lax.all_gather(w_key, "shard", axis=0, tiled=True),
        lax.all_gather(w_value, "shard", axis=0, tiled=True),
        lax.all_gather(w_depth, "shard", axis=1, tiled=True),
        lax.all_gather(w_keyconv, "shard", axis=0, tiled=True),
        lax.all_gather(w_kernel, "shard", axis=1, tiled=True),
        lax.all_gather(w_convout, "shard", axis=0, tiled=True),
        lax.all_gather(w_output, "shard", axis=0, tiled=True),
        lax.all_gather(gain_attn, "shard", axis=0, tiled=True),
        lax.all_gather(w_inter, "shard", axis=2, tiled=True),
        lax.all_gather(w_outer, "shard", axis=1, tiled=True),
        lax.all_gather(gain_ffn, "shard", axis=0, tiled=True),
    )
    saved = layer_forward(seq_rows, segment_ids, params_back)
    hidden_grad, gradients = layer_backward(seq_rows, segment_ids, params_back, saved, cotangent)
    grouped = (
        lax.psum_scatter(gradients[0], "shard", scatter_dimension=0, tiled=True),
        lax.psum_scatter(gradients[1], "shard", scatter_dimension=0, tiled=True),
        lax.psum_scatter(gradients[2], "shard", scatter_dimension=0, tiled=True),
        lax.psum_scatter(gradients[3], "shard", scatter_dimension=1, tiled=True),
        lax.psum_scatter(gradients[4], "shard", scatter_dimension=0, tiled=True),
        lax.psum_scatter(gradients[5], "shard", scatter_dimension=1, tiled=True),
        lax.psum_scatter(gradients[6], "shard", scatter_dimension=0, tiled=True),
        lax.psum_scatter(gradients[7], "shard", scatter_dimension=0, tiled=True),
        lax.psum_scatter(gradients[8], "shard", scatter_dimension=0, tiled=True),
        lax.psum_scatter(gradients[9], "shard", scatter_dimension=2, tiled=True),
        lax.psum_scatter(gradients[10], "shard", scatter_dimension=1, tiled=True),
        lax.psum_scatter(gradients[11], "shard", scatter_dimension=0, tiled=True),
    )
    owner_parts = lax.psum(
        (
            grouped[0],
            grouped[1],
            grouped[2],
            grouped[3],
            grouped[4],
            grouped[5],
            grouped[6],
            grouped[7],
            grouped[8],
            grouped[9],
            grouped[10],
            grouped[11],
        ),
        "rep",
    )
    return (
        output,
        hidden_grad,
        owner_parts[0],
        owner_parts[1],
        owner_parts[2],
        owner_parts[3],
        owner_parts[4],
        owner_parts[5],
        owner_parts[6],
        owner_parts[7],
        owner_parts[8],
        owner_parts[9],
        owner_parts[10],
        owner_parts[11],
    )


def solution(mesh):
    in_specs = (
        P(("rep", "shard"), None),
        P(("rep", "shard"), None),
        P(("rep", "shard"), None),
        P("shard", None),
        P("shard", None),
        P("shard", None),
        P(None, "shard"),
        P("shard", None),
        P(None, "shard"),
        P("shard", None),
        P("shard", None),
        P("shard"),
        P(None, None, "shard"),
        P(None, "shard", None),
        P("shard"),
    )
    out_specs = (
        P(("rep", "shard"), None),
        P(("rep", "shard"), None),
        P("shard", None),
        P("shard", None),
        P("shard", None),
        P(None, "shard"),
        P("shard", None),
        P(None, "shard"),
        P("shard", None),
        P("shard", None),
        P("shard"),
        P(None, None, "shard"),
        P(None, "shard", None),
        P("shard"),
    )
    return jax.shard_map(local, mesh=mesh, in_specs=in_specs, out_specs=out_specs, check_vma=False)
```

profile of v0, /device:TPU:0, one launch (start us, length us, event | category | flops | bytes accessed | tf_op | source)
XLA Modules:
  0.0 921.0 jit_solution(12782089927346242451)
XLA Ops:
  10.7 15.9 %all-gather = bf16[8,96,9]{1,2,0:T(8,128)(2,1)S(1)} all-gather(bf16[1,96,9]{1,2,0:T(8,128)(2,1)} %bitcast.494), channel_id=1, replica_groups=mesh['rep'=4,'shard'=8] {'shard'}, dimensions={0}, use_global_device_ids=true | all-gather | bytes 15552 | tf_op jit(solution)/shard_map/all_gather | solution.py:397
  27.0 14.1 %all_gather.53 = bf16[54,384]{0,1:T(8,128)(2,1)S(1)} all-gather(bf16[54,48]{0,1:T(8,128)(2,1)} %param.29), channel_id=1, replica_groups=mesh['rep'=4,'shard'=8] {'shard'}, dimensions={1}, use_global_device_ids=true | all-gather | bytes 46656 | tf_op jit(solution)/shard_map/all_gather | solution.py:399
  41.1 19.3 %all_gather.48 = bf16[768,384]{1,0:T(8,128)(2,1)} all-gather(bf16[96,384]{1,0:T(8,128)(2,1)} %param.24), channel_id=1, replica_groups=mesh['rep'=4,'shard'=8] {'shard'}, dimensions={0}, use_global_device_ids=true | all-gather | bytes 663552 | tf_op jit(solution)/shard_map/all_gather | solution.py:394
  60.4 18.5 %all_gather.52 = bf16[768,384]{1,0:T(8,128)(2,1)} all-gather(bf16[96,384]{1,0:T(8,128)(2,1)} %param.28), channel_id=1, replica_groups=mesh['rep'=4,'shard'=8] {'shard'}, dimensions={0}, use_global_device_ids=true | all-gather | bytes 663552 | tf_op jit(solution)/shard_map/all_gather | solution.py:398
  79.7 3.4 convolution_convert_fusion.4
  84.8 6.8 fusion.92
  97.7 17.0 %all-reduce.26 = (bf16[768]{0:T(1024)(128)(2,1)S(1)}, bf16[768]{0:T(1024)(128)(2,1)S(1)}) all-reduce(bf16[768]{0:T(1024)(128)(2,1)S(1)} %dynamic-update-slice, bf16[768]{0:T(1024)(128)(2,1)S(1)} %dynamic-update-slice.1), channel_id=1, replica_groups=mesh['rep'=4,'shard'=8] {'shard'}, use_global_device_ids=true, to_apply=%add.19 | all-reduce | flops 1536 | bytes 6144
  117.1 15.1 %all_gather.49 = bf16[768,384]{1,0:T(8,128)(2,1)S(1)} all-gather(bf16[96,384]{1,0:T(8,128)(2,1)S(1)} %copy-done.86), channel_id=1, replica_groups=mesh['rep'=4,'shard'=8] {'shard'}, dimensions={0}, use_global_device_ids=true | all-gather | bytes 663552 | tf_op jit(solution)/shard_map/all_gather | solution.py:395
  132.2 15.3 %all_gather.50 = bf16[768,384]{1,0:T(8,128)(2,1)S(1)} all-gather(bf16[96,384]{1,0:T(8,128)(2,1)S(1)} %copy-done.87), channel_id=1, replica_groups=mesh['rep'=4,'shard'=8] {'shard'}, dimensions={0}, use_global_device_ids=true | all-gather | bytes 663552 | tf_op jit(solution)/shard_map/all_gather | solution.py:396
  147.5 16.5 %all_gather.54 = bf16[768,384]{1,0:T(8,128)(2,1)} all-gather(bf16[96,384]{1,0:T(8,128)(2,1)S(1)} %copy-done.88), channel_id=1, replica_groups=mesh['rep'=4,'shard'=8] {'shard'}, dimensions={0}, use_global_device_ids=true | all-gather | bytes 663552 | tf_op jit(solution)/shard_map/all_gather | solution.py:400
  168.0 59.9 %while.64 = (s32[]{:T(128)}, bf16[2,512,6,64]{1,3,2,0:T(8,128)(2,1)S(1)}, s32[2,512]{1,0:T(2,128)S(1)}, s32[1024]{0:T(1024)S(1)}, bf16[2,512,6,64]{1,3,2,0:T(8,1...) while((s32[]{:T(128)}, ...), condition=%wide.region_3.4_spmd, body=%wide.region_0.3_spmd.sunk | while | flops 830997504 | bytes 54171752 | solution.py:89
  168.4 6.4 fusion.290
  174.8 16.5 %fusion.291 = (f32[6,512]{1,0:T(8,128)S(1)}, f32[6,512,1024]{2,1,0:T(8,128)}) fusion(f32[6,512,1024]{2,1,0:T(8,128)} %fusion.290, pred[512,1024]{1,0:T(8,128)(4,1)S(1)} %broadcast_compare_fusion.6), kind=kOutput, calls=%fused_computation.364.clone.1 | output fusion | flops 18875392 | bytes 25702400 | tf_op jit(solution)/shard_map/while/body/eval_jaxpr/while/body/eval_jaxpr/sub | solution.py:81
  191.3 6.7 fusion.292
  198.3 6.4 fusion.290
  204.7 16.5 %fusion.291 = (f32[6,512]{1,0:T(8,128)S(1)}, f32[6,512,1024]{2,1,0:T(8,128)}) fusion(f32[6,512,1024]{2,1,0:T(8,128)} %fusion.290, pred[512,1024]{1,0:T(8,128)(4,1)S(1)} %broadcast_compare_fusion.6), kind=kOutput, calls=%fused_computation.364.clone.1 | output fusion | flops 18875392 | bytes 25702400 | tf_op jit(solution)/shard_map/while/body/eval_jaxpr/while/body/eval_jaxpr/sub | solution.py:81
  221.2 6.7 fusion.292
  229.8 22.0 %while.65 = (s32[]{:T(128)}, bf16[2,512,6,64]{1,3,2,0:T(8,128)(2,1)S(1)}, f32[2,6,512]{2,1,0:T(8,128)S(1)}, s32[2,512]{1,0:T(2,128)S(1)}, s32[1024]{0:T(1024)S(1...) while((s32[]{:T(128)}, ...), condition=%wide.region_13.14_spmd, body=%wide.region_10.13_spmd.sunk | while | flops 843576320 | bytes 42727540 | solution.py:89
  232.8 3.6 fusion.296
  236.4 4.4 fusion.297
  243.7 3.6 fusion.296
  247.3 4.4 fusion.297
  260.0 7.4 fusion.154
  267.6 3.3 fusion.203
  277.5 5.9 fusion.206
  283.4 4.5 copy-done.3
  288.0 4.0 fusion.48
  292.0 6.1 fusion.207
  304.2 13.1 %add_convert_fusion = bf16[2,1024,1536]{2,1,0:T(8,128)(2,1)} fusion(f32[2,1024,1536]{2,1,0:T(8,128)} %copy-done.3, bf16[1024,2,384]{0,2,1:T(8,128)(2,1)S(1)} %bitcast.481, bf16[2,1536,384]{2,1,0:T(8,128)(2,1)S(1)} %copy-done.141), kind=kOutput, calls=%fused_computation.65 | convolution fusion | flops 2456813568 | bytes 22806528 | tf_op jit(solution)/shard_map/ngd,gfd->ngf/dot_general | solution.py:270
  317.3 5.0 fusion.51
  322.2 5.0 multiply_reduce_fusion.1
  327.2 9.3 %fusion.53 = f32[2,1024,384]{1,2,0:T(8,128)} fusion(bf16[2,1536,384]{2,1,0:T(8,128)(2,1)} %all-gather.9.cloned.1.call-done, bf16[1024,2,384]{0,2,1:T(8,128)(2,1)S(1)} %bitcast.478, bf16[2,384,1536]{1,2,0:T(8,128)(2,1)} %all-gather.7.cloned.1.call-done), kind=kOutput, calls=%fused_computation.85 | convolution fusion | flops 4847566848 | bytes 9437184 | tf_op jit(solution)/shard_map/ngf,gfd->ngd/dot_general | solution.py:209
  336.5 9.0 fusion.190
  349.3 3.3 reshape.1153
  354.7 83.3 %while.66 = (s32[]{:T(128)}, f32[1024,6,64]{0,2,1:T(8,128)S(1)}, f32[1024,6,64]{0,2,1:T(8,128)}, f32[2,512,6,64]{1,0,3,2:T(2,128)}, bf16[2,512,6,64]{1,3,2,0:T(8...) while((s32[]{:T(128)}, f32[1024,6,64]{0,2,1:T(8,128)S(1)}, ...), condition=%wide.region_24.25_spmd.clone, body=%wide.region_22.24_spmd.clone.sunk | while | flops 2063135744 | bytes 117020912 | solution.py:140
  357.1 4.6 bitcast_add_fusion.11
  361.7 7.1 multiply_reduce_fusion.19
  368.8 6.9 multiply_convert_fusion.7
  380.8 15.0 %dynamic_update_slice.39 = f32[2,512,6,64]{1,0,3,2:T(2,128)} dynamic-update-slice(f32[2,512,6,64]{1,0,3,2:T(2,128)} %get-tuple-element.797, f32[1,512,6,64]{1,0,3,2:T(1,128)} %copy.221, s32[]{:T(128)S(6)} %copy.247, s32[]{:T(128)} %constant.134.clone.1..sunk, s32[]{:T(128)} %constant.134.clone.1..sunk, s32[]{:T(128)} %constant.134.clone.1..sunk) | dynamic-update-slice | bytes 1572868 | tf_op jit(solution)/shard_map/while/body/eval_jaxpr/while/body/jit(dynamic_update_index_in_dim)/dynamic_update_slice | solution.py:89
  398.1 5.8 bitcast_add_fusion.11
  403.9 7.1 multiply_reduce_fusion.19
  411.0 6.9 multiply_convert_fusion.7
  422.9 15.0 %dynamic_update_slice.39 = f32[2,512,6,64]{1,0,3,2:T(2,128)} dynamic-update-slice(f32[2,512,6,64]{1,0,3,2:T(2,128)} %get-tuple-element.797, f32[1,512,6,64]{1,0,3,2:T(1,128)} %copy.221, s32[]{:T(128)S(6)} %copy.247, s32[]{:T(128)} %constant.134.clone.1..sunk, s32[]{:T(128)} %constant.134.clone.1..sunk, s32[]{:T(128)} %constant.134.clone.1..sunk) | dynamic-update-slice | bytes 1572868 | tf_op jit(solution)/shard_map/while/body/eval_jaxpr/while/body/jit(dynamic_update_index_in_dim)/dynamic_update_slice | solution.py:89
  440.4 3.2 convolution_bitcast_fusion.1
  455.4 7.8 multiply_reduce_fusion.8
  486.7 3.7 fusion.134
  493.5 4.0 fusion.156
  498.1 4.2 fusion.160
  502.4 9.8 %fusion.209 = f32[2,1536,384]{2,1,0:T(8,128)} fusion(bf16[1024,2,1536]{2,0,1:T(8,128)(2,1)} %fusion.48, bf16[1024,2,384]{0,2,1:T(8,128)(2,1)} %bitcast.482), kind=kOutput, calls=%fused_computation.374 | convolution fusion | flops 2415919104 | bytes 12582912 | tf_op jit(solution)/shard_map/ngf,ngd->gfd/dot_general | solution.py:267
  513.5 8.4 fusion.49
  524.0 7.5 fusion.105
  531.7 9.6 %fusion.115 = (f32[768]{0:T(1024)S(1)}, f32[1,1024,768]{1,2,0:T(8,128)}, f32[1,1024,768]{1,2,0:T(8,128)}, f32[1,1024,768]{1,2,0:T(8,128)}, f32[1,1024,768]{1,2,0...) fusion(bf16[1024,768]{0,1:T(8,128)(2,1)S(1)} %copy-done.10, ...), kind=kLoop, calls=%fused_computation.177 | loop fusion | flops 9436416 | bytes 28339200 | tf_op jit(solution)/shard_map/reduce_sum | solution.py:323
  552.5 25.5 %reduce-scatter.39.cloned.1.call-done = f32[96,384]{1,0:T(8,128)} async-done(((f32[768,384]{1,0:T(8,128)}), f32[96,384]{1,0:T(8,128)}) %reduce-scatter.39.cloned.1.call-update) | async-done | bytes 147472
  579.7 31.8 %reduce-scatter.21.cloned.1.call-done = f32[96,384]{1,0:T(8,128)} async-done(((f32[768,384]{1,0:T(8,128)}), f32[96,384]{1,0:T(8,128)}) %reduce-scatter.21.cloned.1.call-update) | async-done | bytes 147472 | tf_op jit(solution)/shard_map/reduce_scatter | solution.py:430
  611.5 37.7 %reduce-scatter.25.cloned.1.call-done = f32[96,768]{1,0:T(8,128)} async-done(((f32[768,768]{1,0:T(8,128)}), f32[96,768]{1,0:T(8,128)}) %reduce-scatter.25.cloned.1.call-update) | async-done | bytes 294928 | tf_op jit(solution)/shard_map/reduce_scatter | solution.py:433
  649.2 55.9 %reduce-scatter.29.cloned.1.call-done = f32[2,192,384]{2,1,0:T(8,128)} async-done(((f32[2,1536,384]{2,1,0:T(8,128)}), f32[2,192,384]{2,1,0:T(8,128)}) %reduce-scatter.29.cloned.1.call-update) | async-done | bytes 589840 | tf_op jit(solution)/shard_map/reduce_scatter | solution.py:436
  705.1 55.7 %reduce-scatter.27.cloned.1.call-done = f32[2,384,192]{1,2,0:T(8,128)} async-done(((f32[2,384,1536]{1,2,0:T(8,128)}), f32[2,384,192]{1,2,0:T(8,128)}) %reduce-scatter.27.cloned.1.call-update) | async-done | bytes 589840 | tf_op jit(solution)/shard_map/reduce_scatter | solution.py:435
  763.2 14.3 %all-reduce.23 = (f32[768]{0:T(1024)S(1)}, f32[768]{0:T(1024)S(1)}) all-reduce(f32[768]{0:T(1024)S(1)} %copy-done.138, f32[768]{0:T(1024)S(1)} %copy-done.137), channel_id=10, replica_groups=mesh['rep'=4,'shard'=8] {'shard'}, use_global_device_ids=true, to_apply=%region_61.62.clone | all-reduce | flops 1536 | bytes 12288
  780.2 4.1 fusion.210
  786.9 15.5 %fusion.76 = f32[1024,768]{0,1:T(8,128)} fusion(f32[1,1024,768]{1,2,0:T(8,128)} %get-tuple-element.520, f32[1,1024,768]{1,2,0:T(8,128)} %get-tuple-element.513, f32[1,1024,768]{1,2,0:T(8,128)} %get-tuple-element.514, f32[1,1024,768]{1,2,0:T(8,128)} %get-tuple-element.515, f32[1,1024,768]{1,2,0:T(8,128)} %get-tuple-element.516, ...), kind=kOutput, calls=%fused_computation.138 | convolution fusion | flops 622067712 | bytes 43854848 | tf_op jit(solution)/shard_map/dot_general | solution.py:22
  802.5 3.5 copy.117
  806.9 16.8 %reduce-scatter.23.cloned.1.call-done = f32[54,48]{0,1:T(8,128)} async-done(((f32[54,384]{0,1:T(8,128)}), f32[54,48]{0,1:T(8,128)}) %reduce-scatter.23.cloned.1.call-update) | async-done | bytes 10384 | tf_op jit(solution)/shard_map/reduce_scatter | solution.py:431
  823.6 18.1 %all-reduce.24 = (f32[9,96]{1,0:T(8,128)}, f32[54,48]{0,1:T(8,128)}, f32[96]{0:T(128)}, f32[96]{0:T(128)}) all-reduce(f32[9,96]{1,0:T(8,128)S(1)} %copy.142, f32[54,48]{0,1:T(8,128)} %reduce-scatter.23.cloned.1.call-done, f32[96]{0:T(128)S(1)} %dynamic-slice.4, f32[96]{0:T(128)S(1)} %dynamic-slice.6), channel_id=1, replica_groups=mesh['rep'=4,'shard'=8] {'rep'}, use_global_device_ids=true, to_apply=%region_51.52 | all-reduce | flops 3648 | bytes 29184 | tf_op jit(solution)/shard_map/psum | solution.py:439
  841.8 59.6 %all-reduce.29.cloned.1.call-done = (f32[96,384]{0,1:T(8,128)}, f32[96,384]{0,1:T(8,128)}, f32[96,384]{0,1:T(8,128)}, f32[96,384]{1,0:T(8,128)}, f32[96,384]{0,1...) async-done(((f32[96,384]{0,1:T(8,128)}, f32[96,384]{0,1:T(8,128)}, f32[96,384]{0,1:T(8,128)}, f32[96,384]{1,0:T(8,128)}, ...) | async-done | bytes 2211856 | tf_op jit(solution)/shard_map/psum | solution.py:439
  (488 shorter events, 144.5 us)
Async XLA Ops:
  7.2 71.8 %copy-start.16 = (bf16[1024,768]{1,0:T(8,128)(2,1)S(1)}, bf16[1024,768]{1,0:T(8,128)(2,1)}, u32[]{:S(2)}) copy-start(bf16[1024,768]{1,0:T(8,128)(2,1)} %param.21) | copy-start | bytes 4718596
  7.2 260.4 %all-gather.5.cloned.1.call-start = ((), (), s32[]{:S(2)}) async-start(), calls=%async_computation.10 | async-start | bytes 1327104 | tf_op jit(solution)/shard_map/all_gather | solution.py:401
  7.9 269.5 %all-gather.7.cloned.1.call-start = ((), (), s32[]{:S(2)}) async-start(), calls=%async_computation.11 | async-start | bytes 2654208 | tf_op jit(solution)/shard_map/all_gather | solution.py:403
  8.7 283.3 %all-gather.9.cloned.1.call-start = ((), (), s32[]{:S(2)}) async-start(), calls=%async_computation.12 | async-start | bytes 2654208 | tf_op jit(solution)/shard_map/all_gather | solution.py:404
  9.4 538.0 %reduce-scatter.35.cloned.1.call-start = ((), (), s32[]{:S(2)}) async-start(), calls=%async_computation.20 | async-start | bytes 1327104
  10.7 73.9 %copy-start.107 = (pred[1024]{0:T(1024)(128)(4,1)}, pred[1024]{0:T(1024)(128)(4,1)S(1)}, u32[]{:S(2)}) copy-start(pred[1024]{0:T(1024)(128)(4,1)S(1)} %get-tuple-element.416) | copy-start | bytes 3076
  10.7 73.9 %copy-start.111 = (pred[1024]{0:T(1024)(128)(4,1)}, pred[1024]{0:T(1024)(128)(4,1)S(1)}, u32[]{:S(2)}) copy-start(pred[1024]{0:T(1024)(128)(4,1)S(1)} %get-tuple-element.417) | copy-start | bytes 3076
  10.7 73.9 %copy-start.115 = (pred[1024]{0:T(1024)(128)(4,1)}, pred[1024]{0:T(1024)(128)(4,1)S(1)}, u32[]{:S(2)}) copy-start(pred[1024]{0:T(1024)(128)(4,1)S(1)} %get-tuple-element.418) | copy-start | bytes 3076
  10.7 73.9 %copy-start.119 = (pred[1024]{0:T(1024)(128)(4,1)}, pred[1024]{0:T(1024)(128)(4,1)S(1)}, u32[]{:S(2)}) copy-start(pred[1024]{0:T(1024)(128)(4,1)S(1)} %get-tuple-element.419) | copy-start | bytes 3076
  10.7 73.9 %copy-start.123 = (pred[1024]{0:T(1024)(128)(4,1)}, pred[1024]{0:T(1024)(128)(4,1)S(1)}, u32[]{:S(2)}) copy-start(pred[1024]{0:T(1024)(128)(4,1)S(1)} %get-tuple-element.420) | copy-start | bytes 3076
  10.7 73.9 %copy-start.127 = (pred[1024]{0:T(1024)(128)(4,1)}, pred[1024]{0:T(1024)(128)(4,1)S(1)}, u32[]{:S(2)}) copy-start(pred[1024]{0:T(1024)(128)(4,1)S(1)} %get-tuple-element.421) | copy-start | bytes 3076
  10.7 73.9 %copy-start.131 = (pred[1024]{0:T(1024)(128)(4,1)}, pred[1024]{0:T(1024)(128)(4,1)S(1)}, u32[]{:S(2)}) copy-start(pred[1024]{0:T(1024)(128)(4,1)S(1)} %get-tuple-element.422) | copy-start | bytes 3076
  10.7 73.9 %copy-start.134 = (pred[1024]{0:T(1024)(128)(4,1)}, pred[1024]{0:T(1024)(128)(4,1)S(1)}, u32[]{:S(2)}) copy-start(pred[1024]{0:T(1024)(128)(4,1)S(1)} %get-tuple-element.423) | copy-start | bytes 3076
  26.9 57.8 %copy-start.89 = (f32[768]{0:T(1024)}, f32[768]{0:T(1024)S(1)}, u32[]{:S(2)}) copy-start(f32[768]{0:T(1024)S(1)} %get-tuple-element.412) | copy-start | bytes 9220
  26.9 57.8 %copy-start.91 = (f32[768]{0:T(1024)}, f32[768]{0:T(1024)S(1)}, u32[]{:S(2)}) copy-start(f32[768]{0:T(1024)S(1)} %get-tuple-element.407) | copy-start | bytes 9220
  26.9 57.8 %copy-start.93 = (f32[768]{0:T(1024)}, f32[768]{0:T(1024)S(1)}, u32[]{:S(2)}) copy-start(f32[768]{0:T(1024)S(1)} %get-tuple-element.408) | copy-start | bytes 9220
  26.9 57.8 %copy-start.95 = (f32[768]{0:T(1024)}, f32[768]{0:T(1024)S(1)}, u32[]{:S(2)}) copy-start(f32[768]{0:T(1024)S(1)} %get-tuple-element.409) | copy-start | bytes 9220
  26.9 57.8 %copy-start.97 = (f32[768]{0:T(1024)}, f32[768]{0:T(1024)S(1)}, u32[]{:S(2)}) copy-start(f32[768]{0:T(1024)S(1)} %get-tuple-element.410) | copy-start | bytes 9220
  26.9 57.8 %copy-start.99 = (f32[768]{0:T(1024)}, f32[768]{0:T(1024)S(1)}, u32[]{:S(2)}) copy-start(f32[768]{0:T(1024)S(1)} %get-tuple-element.411) | copy-start | bytes 9220
  26.9 57.8 %copy-start.101 = (f32[768]{0:T(1024)}, f32[768]{0:T(1024)S(1)}, u32[]{:S(2)}) copy-start(f32[768]{0:T(1024)S(1)} %get-tuple-element.413) | copy-start | bytes 9220
  26.9 57.8 %copy-start.103 = (f32[768]{0:T(1024)}, f32[768]{0:T(1024)S(1)}, u32[]{:S(2)}) copy-start(f32[768]{0:T(1024)S(1)} %get-tuple-element.414) | copy-start | bytes 9220
  27.0 57.8 %copy-start.105 = (f32[768]{0:T(1024)}, f32[768]{0:T(1024)S(1)}, u32[]{:S(2)}) copy-start(f32[768]{0:T(1024)S(1)} %get-tuple-element.415) | copy-start | bytes 9220
  41.1 51.6 %copy-start.56 = (bf16[54,384]{0,1:T(8,128)(2,1)}, bf16[54,384]{0,1:T(8,128)(2,1)S(1)}, u32[]{:S(2)}) copy-start(bf16[54,384]{0,1:T(8,128)(2,1)S(1)} %all_gather.53) | copy-start | bytes 124420
  79.7 11.9 %copy-start.7 = (bf16[1024,768]{0,1:T(8,128)(2,1)}, bf16[1024,768]{0,1:T(8,128)(2,1)S(1)}, u32[]{:S(2)}) copy-start(bf16[1024,768]{0,1:T(8,128)(2,1)S(1)} %copy.94) | copy-start | bytes 4718596
  83.1 8.5 copy-start.61
  93.9 21.9 %copy-start.55 = (s32[1,1024]{1,0:T(1,128)S(1)}, s32[1,1024]{1,0:T(1,128)}, u32[]{:S(2)}) copy-start(s32[1,1024]{1,0:T(1,128)} %param.22) | copy-start | bytes 12292
  93.9 23.2 %copy-start.86 = (bf16[96,384]{1,0:T(8,128)(2,1)S(1)}, bf16[96,384]{1,0:T(8,128)(2,1)}, u32[]{:S(2)}) copy-start(bf16[96,384]{1,0:T(8,128)(2,1)} %param.25) | copy-start | bytes 221188
  94.0 38.3 %copy-start.87 = (bf16[96,384]{1,0:T(8,128)(2,1)S(1)}, bf16[96,384]{1,0:T(8,128)(2,1)}, u32[]{:S(2)}) copy-start(bf16[96,384]{1,0:T(8,128)(2,1)} %param.26) | copy-start | bytes 221188
  94.0 53.5 %copy-start.88 = (bf16[96,384]{1,0:T(8,128)(2,1)S(1)}, bf16[96,384]{1,0:T(8,128)(2,1)}, u32[]{:S(2)}) copy-start(bf16[96,384]{1,0:T(8,128)(2,1)} %param.30) | copy-start | bytes 221188
  94.4 69.7 %copy-start.42 = (f32[1024,54]{0,1:T(8,128)}, f32[1024,54]{0,1:T(8,128)S(1)}, u32[]{:S(2)}) copy-start(f32[1024,54]{0,1:T(8,128)S(1)} %fusion.187) | copy-start | bytes 663556
  132.2 34.8 %copy-start.49 = (bf16[768,384]{1,0:T(8,128)(2,1)}, bf16[768,384]{1,0:T(8,128)(2,1)S(1)}, u32[]{:S(2)}) copy-start(bf16[768,384]{1,0:T(8,128)(2,1)S(1)} %all_gather.49) | copy-start | bytes 1769476
  147.5 19.6 %copy-start.47 = (bf16[768,384]{1,0:T(8,128)(2,1)}, bf16[768,384]{1,0:T(8,128)(2,1)S(1)}, u32[]{:S(2)}) copy-start(bf16[768,384]{1,0:T(8,128)(2,1)S(1)} %all_gather.50) | copy-start | bytes 1769476
  258.8 8.6 copy-start.64
  258.9 8.6 copy-start.66
  258.9 8.6 copy-start.68
  258.9 8.6 copy-start.70
  258.9 8.6 copy-start.72
  259.0 8.5 copy-start.74
  259.0 8.5 copy-start.76
  259.0 8.5 copy-start.78
  259.0 8.5 copy-start.80
  304.2 13.1 %copy-start.50 = (bf16[2,384,1536]{1,2,0:T(8,128)(2,1)S(1)}, bf16[2,384,1536]{1,2,0:T(8,128)(2,1)}, u32[]{:S(2)}) copy-start(bf16[2,384,1536]{1,2,0:T(8,128)(2,1)} %all-gather.7.cloned.1.call-done) | copy-start | bytes 7077892
  336.5 9.1 copy-start.143
  446.4 102.7 %reduce-scatter.33.cloned.1.call-start = ((), (), s32[]{:S(2)}) async-start(), calls=%async_computation.19 | async-start | bytes 1327104
  452.3 98.5 %reduce-scatter.31.cloned.1.call-start = ((), (), s32[]{:S(2)}) async-start(), calls=%async_computation.18 | async-start | bytes 1327104
  455.4 8.5 copy-start.51
  464.2 9.8 %copy-start.35 = (f32[1,1024,6,9]{1,3,2,0:T(8,128)S(1)}, f32[1,1024,6,9]{1,3,2,0:T(8,128)}, u32[]{:S(2)}) copy-start(f32[1,1024,6,9]{1,3,2,0:T(8,128)} %reshape.1135) | copy-start | bytes 663556
  465.8 10.6 %copy-start.22 = (f32[1024,384]{1,0:T(8,128)S(1)}, f32[1024,384]{1,0:T(8,128)}, u32[]{:S(2)}) copy-start(f32[1024,384]{1,0:T(8,128)} %copy-done.21) | copy-start | bytes 4718596
  484.8 93.2 %reduce-scatter.39.cloned.1.call-start = ((), (), s32[]{:S(2)}) async-start(), calls=%async_computation.22 | async-start | bytes 1327104
  493.5 118.0 %reduce-scatter.21.cloned.1.call-start = ((), (), s32[]{:S(2)}) async-start(), calls=%async_computation.13 | async-start | bytes 1327104 | tf_op jit(solution)/shard_map/reduce_scatter | solution.py:430
  497.6 151.6 %reduce-scatter.25.cloned.1.call-start = ((), (), s32[]{:S(2)}) async-start(), calls=%async_computation.15 | async-start | bytes 2654208 | tf_op jit(solution)/shard_map/reduce_scatter | solution.py:433
  502.3 202.8 %reduce-scatter.29.cloned.1.call-start = ((), (), s32[]{:S(2)}) async-start(), calls=%async_computation.17 | async-start | bytes 5308416 | tf_op jit(solution)/shard_map/reduce_scatter | solution.py:436
  512.2 248.7 %reduce-scatter.27.cloned.1.call-start = ((), (), s32[]{:S(2)}) async-start(), calls=%async_computation.16 | async-start | bytes 5308416 | tf_op jit(solution)/shard_map/reduce_scatter | solution.py:435
  522.1 283.9 %reduce-scatter.37.cloned.1.call-start = ((), (), s32[]{:S(2)}) async-start(), calls=%async_computation.21 | async-start | bytes 442368
  523.9 7.7 copy-start.10
  523.9 7.7 copy-start.92
  523.9 7.7 copy-start.94
  523.9 7.7 copy-start.96
  531.4 9.8 %copy-start.32 = (bf16[1024,768]{0,1:T(8,128)(2,1)}, bf16[1024,768]{0,1:T(8,128)(2,1)S(1)}, u32[]{:S(2)}) copy-start(bf16[1024,768]{0,1:T(8,128)(2,1)S(1)} %get-tuple-element.550) | copy-start | bytes 4718596
  531.6 10.6 %copy-start.139 = (f32[1024]{0:T(1024)S(1)}, f32[1024]{0:T(1024)}, u32[]{:S(2)}) copy-start(f32[1024]{0:T(1024)} %get-tuple-element.495) | copy-start | bytes 12292
  531.6 10.6 %copy-start.4 = (f32[1024,768]{0,1:T(8,128)S(1)}, f32[1024,768]{0,1:T(8,128)}, u32[]{:S(2)}) copy-start(f32[1024,768]{0,1:T(8,128)} %get-tuple-element.496) | copy-start | bytes 9437188
  545.0 278.6 %reduce-scatter.23.cloned.1.call-start = ((), (), s32[]{:S(2)}) async-start(), calls=%async_computation.14 | async-start | bytes 221184 | tf_op jit(solution)/shard_map/reduce_scatter | solution.py:431
  545.8 355.6 %all-reduce.29.cloned.1.call-start = ((), (), s32[]{:S(2)}) async-start(), calls=%async_computation.23 | async-start | bytes 4816896 | tf_op jit(solution)/shard_map/psum | solution.py:439
  901.3 12.1 %copy-start.62 = (f32[2,192,384]{2,1,0:T(8,128)S(1)}, f32[2,192,384]{2,1,0:T(8,128)}, u32[]{:S(2)}) copy-start(f32[2,192,384]{2,1,0:T(8,128)} %get-tuple-element.832) | copy-start | bytes 1769476
  (98 other events, 309.2 us)
Sparse Core Ops, SparseCore 0:
  9.6 25.6 all-gather.4
  36.9 37.8 all-gather.6
  76.4 31.1 all-gather.8
  446.5 31.3 reduce-scatter.34
  480.0 31.2 reduce-scatter.32
  513.4 31.1 reduce-scatter.30
  546.9 31.1 reduce-scatter.38
  580.3 31.1 reduce-scatter.20
  613.9 35.3 reduce-scatter.24
  651.4 53.7 reduce-scatter.28
  707.4 53.3 reduce-scatter.26
  762.9 29.6 reduce-scatter.36
  794.8 28.7 reduce-scatter.22
  828.0 73.2 all-reduce.28
where the time goes:
time: 932 us; the launch traced here: 921 us
  waiting for transfers between devices  286 us (31%)
  matrix products  201 us (22%)
  blocking collectives  164 us (18%)
  other arithmetic  127 us (14%)
  local copies, waits for them, and re-layouts  124 us (13%)
  between operations  17.7 us (2%)
    unnamed x328, local copies, waits for them, and re-layouts  67.7 us
    psum x1, waiting for transfers between devices, local(): lax.psum((grouped[0], grouped[1], grouped[2], grouped[3], grouped[4], gro...  59.6 us
    reduce_scatter x1, waiting for transfers between devices, local(): lax.psum_scatter(gradients[10], 'shard', scatter_dimension=1, tiled=True)  55.9 us
    reduce_scatter x1, waiting for transfers between devices, local(): lax.psum_scatter(gradients[9], 'shard', scatter_dimension=2, tiled=True)  55.7 us
    reduce_scatter x1, waiting for transfers between devices, local(): lax.psum_scatter(gradients[7], 'shard', scatter_dimension=0, tiled=True)  37.7 us
    dot_general x7, matrix products, product_nt(): lax.dot_general(left, right, (((1,), (1,)), ((), ())), preferred_element_...  33.8 us
    dynamic_update_slice x4, local copies, waits for them, and re-layouts, attend_forward(): lax.map(one_block, (queries_seq.reshape(count, block, heads, head_size),...  33.4 us
    sub x2, other arithmetic, one_block(): weights = jnp.exp(scores - row_top)  33 us
  transfers between devices with their start and end apart: 14, of which 7 were waited for; matrix products, arithmetic and copies ran while one was open for 29% of the time, Pallas kernels for 0%

commit v1 on v0

v1 whole, which is shorter than its diff:
```python
import functools
import math

import jax
import jax.numpy as jnp
from jax import lax
from jax.experimental import pallas as pl
from jax.experimental.pallas import tpu as pltpu
from jax.sharding import PartitionSpec as P

f32 = jnp.float32
bf16 = jnp.bfloat16
EPS = 1e-05
FAR = 1e9
WIDTH = 384
LANES = 128
SLOT = 8
BLK = 256
AUG = 16
INV_SQRT2 = 0.7071067811865476
INV_SQRT2PI = 0.3989422804014327


def dg(left, right, cl, cr):
    return lax.dot_general(
        left, right, (((cl,), (cr,)), ((), ())), preferred_element_type=f32
    )


def up(value, unit):
    return -(-value // unit) * unit


class Plan:
    def __init__(self, shards, model, att, ff_rows, groups):
        self.shards = shards
        self.rows_in = model // shards
        self.rows_ff = ff_rows // shards
        self.rows_small = up(att // shards, 16)
        self.n_small = att // shards
        self.offset = {}
        self.count = {}
        at = 0
        for name, n in (
            [(k, self.rows_in) for k in ("query", "key", "value", "keyconv", "convout")]
            + [("small", self.rows_small)]
            + [("out0", self.rows_in), ("out1", self.rows_in)]
            + [("inter%d" % g, self.rows_ff) for g in range(groups)]
            + [("outer%d" % g, self.rows_ff) for g in range(groups)]
        ):
            self.offset[name] = at
            self.count[name] = n
            at += n
        self.rows = at


FRONT = ("query", "key", "value", "keyconv", "convout", "small")


def mega(
    plan, heads, taps, length, model,
    hid, cot, segr, gath,
    out_ref, hg, grads, probs_hbm,
    wts, smalls, segb, cmf, qaT, kaT, vaT, qs, cvf, tw, depth_low, kc, mixed,
    ctx, attT, linv, prob, expand, gn, dout, stage, dsem,
):
    half = (taps - 1) // 2
    att = heads * (WIDTH // heads)
    hs = att // heads
    groups = model // WIDTH
    cols_m = model // LANES
    cols_a = att // LANES
    nblk = length // BLK
    PADR = 8
    span = taps * LANES

    names = list(FRONT) + [n for n in plan.offset if n not in FRONT]
    wcopies = {}
    for i, name in enumerate(names):
        dst = smalls if name == "small" else wts[name]
        wcopies[name] = pltpu.make_async_copy(
            gath.at[:, pl.ds(plan.offset[name], plan.count[name]), :], dst, dsem.at[i]
        )
        wcopies[name].start()

    part = plan.shards // 2
    nff = plan.shards * plan.rows_ff

    def weight(name, k=None):
        ref = wts[name]
        value = ref[...] if k is None else ref[k * part:(k + 1) * part]
        return value.reshape(value.shape[0] * value.shape[1], WIDTH)

    def rows_of(b):
        return pl.ds(pl.multiple_of(b * BLK, BLK), BLK)

    def blocks(body, n=nblk):
        def step(b, carry):
            body(b)
            return carry
        lax.fori_loop(0, n, step, 0)

    segf = segr[...].astype(f32)
    wide = jnp.broadcast_to(segf, (LANES, length)).T
    edge = jnp.full((PADR, LANES), -1.0, f32)
    segb[0:PADR, :] = edge
    segb[PADR + length:, :] = edge
    segb[pl.ds(PADR, length), :] = wide

    def pad_edges(ref):
        for c in range(ref.shape[0]):
            ref[c, 0:PADR, :] = jnp.zeros((PADR, LANES), f32)
            ref[c, PADR + length:, :] = jnp.zeros((PADR, LANES), f32)
    pad_edges(cvf)

    def masks(b):
        base = pl.multiple_of(b * BLK, BLK)
        own = segb[pl.ds(base + PADR, BLK), :]
        slot = lax.broadcasted_iota(jnp.int32, (BLK, LANES), 1) // SLOT
        acc = jnp.zeros((BLK, LANES), f32)
        for t in range(taps):
            same = segb[pl.ds(base + PADR + t - half, BLK), :] == own
            acc = jnp.where((slot == t) & same, 1.0, acc)
        cmf[rows_of(b), :] = acc
    blocks(masks)

    iota_r = lax.broadcasted_iota(jnp.int32, (2 * LANES, LANES), 0) % LANES
    iota_c = lax.broadcasted_iota(jnp.int32, (2 * LANES, LANES), 1)
    for c in range(cols_a):
        for t in range(taps):
            want = t * SLOT + (c * LANES + iota_c) // hs
            expand[:, c * span + t * LANES:c * span + (t + 1) * LANES] = jnp.where(
                iota_r == want, 1.0, 0.0
            ).astype(bf16)

    lane16 = lax.broadcasted_iota(jnp.int32, (AUG, length), 0).astype(f32)
    seg16 = jnp.broadcast_to(segf, (AUG, length))
    q_extra = jnp.where(lane16 == seg16, 0.0, jnp.where(lane16 < 8.0, -FAR, 0.0)).astype(bf16)
    k_extra = jnp.where(lane16 == seg16, 1.0, 0.0).astype(bf16)
    v_extra = jnp.where(lane16 < 3.0, 1.0, 0.0).astype(bf16)
    for h in range(heads):
        qaT[h, hs:, :] = q_extra
        kaT[h, hs:, :] = k_extra
        vaT[h, hs:, :] = v_extra

    wcopies["small"].wait()
    ns = plan.n_small
    wkT = jnp.concatenate(
        [smalls[s, :, 0:LANES].astype(f32)[0:ns] for s in range(plan.shards)], axis=0
    ).astype(bf16)
    per_feature = jnp.concatenate(
        [
            smalls[s, :, (1 + j) * LANES:(2 + j) * LANES].astype(f32)[0:ns]
            for s in range(plan.shards)
            for j in range(2)
        ],
        axis=0,
    )
    gn[0:AUG, :] = per_feature.T[0:AUG, :]
    gain_a = gn[taps:taps + 1, :]
    gain_f = gn[taps + 1:taps + 2, :]

    CH = 64

    def depth_scope(xf):
        pad_edges(xf)

        def fill(b):
            base = pl.multiple_of(b * BLK, BLK)
            for c in range(cols_m):
                xf[c, pl.ds(base + PADR, BLK), :] = hid[rows_of(b), c * LANES:(c + 1) * LANES].astype(f32)
        blocks(fill)

        def depth_chunk(b, carry):
            base = pl.multiple_of(b * CH, CH)
            own = segb[pl.ds(base + PADR, CH), :]
            accs = [jnp.zeros((CH, LANES), f32) for _ in range(cols_m)]
            for t in range(taps):
                at = base + PADR + t - half
                same = segb[pl.ds(at, CH), :] == own
                for c in range(cols_m):
                    tap = gn[t:t + 1, c * LANES:(c + 1) * LANES]
                    accs[c] = accs[c] + jnp.where(same, xf[c, pl.ds(at, CH), :], 0.0) * tap
            for c in range(cols_m):
                depth_low[pl.ds(base, CH), c * LANES:(c + 1) * LANES] = accs[c].astype(bf16)
            return carry
        lax.fori_loop(0, length // CH, depth_chunk, 0)
    pl.run_scoped(depth_scope, pltpu.VMEM((cols_m, length + 2 * PADR, LANES), f32))

    for name in ("query", "key", "value", "convout", "keyconv"):
        wcopies[name].wait()

    def project(b):
        r = rows_of(b)
        rows = hid[r, :]
        q = dg(rows, weight("query"), 1, 0).astype(bf16)
        qs[r, :] = q
        qT = (q.astype(f32) * (hs ** -0.5)).astype(bf16).T
        kT = dg(rows, weight("key"), 1, 0).astype(bf16).T
        vT = dg(rows, weight("value"), 1, 0).astype(bf16).T
        for h in range(heads):
            qaT[h, 0:hs, r] = qT[h * hs:(h + 1) * hs]
            kaT[h, 0:hs, r] = kT[h * hs:(h + 1) * hs]
            vaT[h, 0:hs, r] = vT[h * hs:(h + 1) * hs]
        cv = dg(rows, weight("convout"), 1, 0)
        for c in range(cols_a):
            cvf[c, pl.ds(pl.multiple_of(b * BLK, BLK) + PADR, BLK), :] = cv[:, c * LANES:(c + 1) * LANES]
        keyconv = dg(depth_low[r, :], weight("keyconv"), 1, 0)
        kc[r, :] = keyconv
        mk = (keyconv * q.astype(f32)).astype(bf16)
        mixed[r, :] = mk
        logits = dg(mk, wkT, 1, 0)
        lane = lax.broadcasted_iota(jnp.int32, logits.shape, 1)
        logits = jnp.where(lane < taps * SLOT, logits, -1e30)
        top = logits
        for s in (64, 32, 16, 8):
            top = jnp.maximum(top, pltpu.roll(top, b * 0 + s, 1))
        e = jnp.exp(logits - top)
        total = e
        for s in (64, 32, 16, 8):
            total = total + pltpu.roll(total, b * 0 + s, 1)
        tw[r, :] = e / total
    blocks(project)

    def split(value):
        high = value.astype(bf16)
        low = (value - high.astype(f32)).astype(bf16)
        return jnp.concatenate([high, low], axis=1)

    CV = 128

    def conv_chunk(b, carry):
        base = pl.multiple_of(b * CV, CV)
        r = pl.ds(base, CV)
        pair = split(tw[r, :] * cmf[r, :])
        for c in range(cols_a):
            big = dg(pair, expand[:, c * span:(c + 1) * span], 1, 0)
            acc = jnp.zeros((CV, LANES), f32)
            for t in range(taps):
                acc = acc + big[:, t * LANES:(t + 1) * LANES] * cvf[c, pl.ds(base + PADR + t - half, CV), :]
            ctx[r, att + c * LANES:att + (c + 1) * LANES] = acc.astype(bf16)
        return carry
    lax.fori_loop(0, length // CV, conv_chunk, 0)

    def p_out(h):
        return pltpu.make_async_copy(prob.at[h % 2], probs_hbm.at[h], dsem.at[len(names) + h % 2])

    for h in range(heads):
        if 2 <= h:
            p_out(h - 2).wait()

        def fwd(b, h=h):
            r = rows_of(b)
            s = dg(qaT[h, :, r], kaT[h], 0, 0)
            top = jnp.max(s, axis=1, keepdims=True)
            e = jnp.exp(s - top).astype(bf16)
            prob[h % 2, r, :] = e
            o = dg(vaT[h], e, 1, 1)
            inv = 1.0 / o[hs:hs + 1, :]
            linv[h:h + 1, r] = inv
            attT[h * hs:(h + 1) * hs, r] = o[0:hs, :] * inv
        blocks(fwd)
        if h < heads - 2:
            p_out(h).start()

    def to_ctx(b):
        r = rows_of(b)
        ctx[r, 0:att] = attT[:, r].astype(bf16).T
    blocks(to_ctx)

    for name in names:
        if name not in FRONT:
            wcopies[name].wait()

    def norm_back(grad, unit, scale, gain):
        e = grad * gain
        inside = e - jnp.mean(e, axis=1, keepdims=True) - unit * jnp.mean(e * unit, axis=1, keepdims=True)
        return scale * inside

    send = {}

    def outgoing(name, slot):
        n = plan.count[name]
        return pltpu.make_async_copy(
            stage.at[slot, pl.ds(0, plan.shards * n)].reshape(plan.shards, n, WIDTH),
            grads.at[:, pl.ds(plan.offset[name], n), :],
            dsem.at[len(names) + 2 + slot],
        )

    def drain(slot):
        if slot in send:
            outgoing(send.pop(slot), slot).wait()

    def ship(name, value, slot):
        drain(slot)
        stage[slot, 0:plan.shards * plan.count[name], :] = value.astype(bf16)
        outgoing(name, slot).start()
        send[slot] = name

    def mid_scope(act, dinner, nl, db, slope):
        gn[AUG:AUG + 2 * SLOT, :] = jnp.zeros((2 * SLOT, model), f32)

        def mid(b):
            r = rows_of(b)
            c = ctx[r, :]
            first = jnp.concatenate(
                [dg(c, weight("out%d" % j), 1, 0) for j in range(groups)], axis=1
            ) + hid[r, :].astype(f32)
            cen = first - jnp.mean(first, axis=1, keepdims=True)
            s1 = lax.rsqrt(jnp.mean(cen * cen, axis=1, keepdims=True) + EPS)
            unit1 = cen * s1
            normed = unit1 * gain_a
            low = normed.astype(bf16)
            nl[r, :] = low
            ffs = []
            for g in range(groups):
                total = jnp.zeros((BLK, WIDTH), f32)
                for k in range(plan.shards // part):
                    inner = dg(low[:, g * WIDTH:(g + 1) * WIDTH], weight("inter%d" % g, k), 1, 1)
                    at = g * nff + k * inner.shape[1]
                    phi = 0.5 + 0.5 * lax.erf(inner * INV_SQRT2)
                    a = (inner * phi).astype(bf16)
                    act[r, at:at + inner.shape[1]] = a
                    slope[:, at:at + inner.shape[1]] = (
                        phi + inner * jnp.exp(inner * inner * -0.5) * INV_SQRT2PI
                    ).astype(bf16)
                    total = total + dg(a, weight("outer%d" % g, k), 1, 0)
                ffs.append(total)
            second = jnp.concatenate(ffs, axis=1) + normed
            cen2 = second - jnp.mean(second, axis=1, keepdims=True)
            s2 = lax.rsqrt(jnp.mean(cen2 * cen2, axis=1, keepdims=True) + EPS)
            unit2 = cen2 * s2
            out_ref[r, :] = (unit2 * gain_f).astype(bf16)
            dy = cot[r, :].astype(f32)
            gn[AUG:AUG + SLOT, :] += jnp.sum((dy * unit2).reshape(BLK // SLOT, SLOT, model), axis=0)
            dsec = norm_back(dy, unit2, s2, gain_f)
            dlow = dsec.astype(bf16)
            db[r, :] = dlow
            backs = []
            for g in range(groups):
                total = jnp.zeros((BLK, WIDTH), f32)
                for k in range(plan.shards // part):
                    da = dg(dlow[:, g * WIDTH:(g + 1) * WIDTH], weight("outer%d" % g, k), 1, 1)
                    at = g * nff + k * da.shape[1]
                    di = (da * slope[:, at:at + da.shape[1]].astype(f32)).astype(bf16)
                    dinner[r, at:at + da.shape[1]] = di
                    total = total + dg(di, weight("inter%d" % g, k), 1, 0)
                backs.append(total)
            dn = dsec + jnp.concatenate(backs, axis=1)
            gn[AUG + SLOT:AUG + 2 * SLOT, :] += jnp.sum((dn * unit1).reshape(BLK // SLOT, SLOT, model), axis=0)
            dfirst = norm_back(dn, unit1, s1, gain_a)
            hg[r, :] = dfirst
            do = dfirst.astype(bf16)
            dout[r, :] = do
        blocks(mid)

        for g in range(groups):
            cols = slice(g * WIDTH, (g + 1) * WIDTH)
            for slot, (name, left, right) in enumerate((("outer", act, db), ("inter", dinner, nl))):
                drain(slot)
                for k in range(4):
                    n = nff // 4
                    at = g * nff + k * n
                    stage[slot, k * n:(k + 1) * n, :] = dg(left[:, at:at + n], right[:, cols], 0, 0).astype(bf16)
                outgoing("%s%d" % (name, g), slot).start()
                send[slot] = "%s%d" % (name, g)

    ff = 2 * plan.rows_ff * plan.shards
    pl.run_scoped(
        mid_scope,
        pltpu.VMEM((length, ff), bf16),
        pltpu.VMEM((length, ff), bf16),
        pltpu.VMEM((length, model), bf16),
        pltpu.VMEM((length, model), bf16),
        pltpu.VMEM((BLK, ff), bf16),
    )

    def back_scope(xf, doaT, dS, dall, dkc, dlog, dcv, prod, gd):
        for j in range(groups):
            ship("out%d" % j, dg(ctx[...], dout[:, j * WIDTH:(j + 1) * WIDTH], 0, 0), j % 2)

        def dctx(b):
            r = rows_of(b)
            d = dout[r, :]
            full = sum(
                dg(d[:, j * WIDTH:(j + 1) * WIDTH], weight("out%d" % j), 1, 1) for j in range(groups)
            ).astype(bf16)
            ctx[r, att:] = full[:, att:]
            dT = full[:, 0:att].T.astype(f32)
            for h in range(heads):
                scaled = (dT[h * hs:(h + 1) * hs] * linv[h:h + 1, r]).astype(bf16)
                doaT[h, 0:hs, r] = scaled
                drop = -jnp.sum(scaled.astype(f32) * attT[h * hs:(h + 1) * hs, r], axis=0, keepdims=True)
                d1 = drop.astype(bf16).astype(f32)
                d2 = (drop - d1).astype(bf16).astype(f32)
                d3 = drop - d1 - d2
                line = lax.broadcasted_iota(jnp.int32, (AUG, BLK), 0)
                extra = jnp.where(line == 0, d1, jnp.where(line == 1, d2, jnp.where(line == 2, d3, 0.0)))
                doaT[h, hs:, r] = extra.astype(bf16)
        blocks(dctx)

        order = [heads - 2, heads - 1] + list(range(heads - 2))

        def p_in(h, slot):
            return pltpu.make_async_copy(probs_hbm.at[h], prob.at[slot], dsem.at[len(names) + slot])

        for i, h in enumerate(order):
            slot = i % 2 if heads % 2 == 0 else (heads - 2 + i) % 2
            if i >= 2:
                p_in(h, slot).wait()

            def bwd(b, h=h, slot=slot):
                r = rows_of(b)
                dp = dg(doaT[h, :, r], vaT[h], 0, 0)
                dS[r, :] = (prob[slot, r, :].astype(f32) * dp).astype(bf16)
            blocks(bwd)
            dqT = dg(kaT[h, 0:hs, :], dS[...], 1, 1) * (hs ** -0.5)
            dkT = dg(qaT[h, 0:hs, :], dS[...], 1, 0)
            dvT = dg(doaT[h, 0:hs, :], prob[slot], 1, 0)
            attT[h * hs:(h + 1) * hs, :] = dqT
            kaT[h, 0:hs, :] = dkT.astype(bf16)
            vaT[h, 0:hs, :] = dvT.astype(bf16)
            if i + 2 < heads:
                p_in(order[i + 2], slot).start()

        pad_edges(xf)
        for c in range(cols_a):
            dcv[c, :, :] = jnp.zeros((length + 2 * PADR, LANES), f32)

        def conv_back(b, carry):
            base = pl.multiple_of(b * CV, CV)
            r = pl.ds(base, CV)
            w = tw[r, :]
            mask = cmf[r, :]
            pair = split(w * mask)
            dt = jnp.zeros((CV, LANES), f32)
            for c in range(cols_a):
                dc = ctx[r, att + c * LANES:att + (c + 1) * LANES].astype(f32)
                big = dg(pair, expand[:, c * span:(c + 1) * span], 1, 0)
                for t in range(taps):
                    at = base + PADR + t - half
                    prod[:, t * LANES:(t + 1) * LANES] = (dc * cvf[c, pl.ds(at, CV), :]).astype(bf16)
                    dcv[c, pl.ds(at, CV), :] += big[:, t * LANES:(t + 1) * LANES] * dc
                dt = dt + dg(prod[...], expand[0:LANES, c * span:(c + 1) * span], 1, 1)
            dt = dt * mask
            total = dt * w
            for s in (64, 32, 16, 8):
                total = total + pltpu.roll(total, b * 0 + s, 1)
            dl = (w * (dt - total)).astype(bf16)
            dlog[r, :] = dl
            dm = dg(dl, wkT, 1, 1).astype(bf16).astype(f32)
            dkc[r, :] = (dm * qs[r, :].astype(f32)).astype(bf16)
            kc[r, :] = dm * kc[r, :]
            return carry
        lax.fori_loop(0, length // CV, conv_back, 0)

        def collect(b):
            r = rows_of(b)
            at = pl.multiple_of(b * BLK, BLK) + PADR
            dall[r, 0:att] = (attT[:, r].T + kc[r, :]).astype(bf16)
            for h in range(heads):
                pass
            kk = jnp.concatenate([kaT[h, 0:hs, r] for h in range(heads)], axis=0)
            vv = jnp.concatenate([vaT[h, 0:hs, r] for h in range(heads)], axis=0)
            dall[r, att:2 * att] = kk.T
            dall[r, 2 * att:3 * att] = vv.T
            for c in range(cols_a):
                dall[r, 3 * att + c * LANES:3 * att + (c + 1) * LANES] = dcv[c, pl.ds(at, BLK), :].astype(bf16)
            dd = dg(dkc[r, :], weight("keyconv"), 1, 1).astype(bf16).astype(f32)
            for c in range(cols_m):
                xf[c, pl.ds(at, BLK), :] = dd[:, c * LANES:(c + 1) * LANES]
            total = hg[r, :]
            for j, name in enumerate(("query", "key", "value", "convout")):
                total = total + dg(dall[r, j * att:(j + 1) * att], weight(name), 1, 1)
            hg[r, :] = total
        blocks(collect)

        ship("keyconv", dg(depth_low[...], dkc[...], 0, 0), 0)
        for j, name in enumerate(("query", "key", "value", "convout")):
            ship(name, dg(hid[...], dall[:, j * att:(j + 1) * att], 0, 0), (j + 1) % 2)

        gk = dg(mixed[...], dlog[...], 0, 0)

        gd[...] = jnp.zeros(gd.shape, f32)

        def depth_back(b, carry):
            base = pl.multiple_of(b * CH, CH)
            own = segb[pl.ds(base + PADR, CH), :]
            r = pl.ds(base, CH)
            sames = [segb[pl.ds(base + PADR + t - half, CH), :] == own for t in range(taps)]
            for c in range(cols_m):
                lanes = slice(c * LANES, (c + 1) * LANES)
                x = hid[r, lanes].astype(f32)
                acc = hg[r, lanes]
                for t in range(taps):
                    back = taps - 1 - t
                    v = jnp.where(sames[t], xf[c, pl.ds(base + PADR + t - half, CH), :], 0.0)
                    acc = acc + v * gn[back:back + 1, lanes]
                    gd[back, :, lanes] += jnp.sum((v * x).reshape(CH // SLOT, SLOT, LANES), axis=0)
                hg[r, lanes] = acc
            return carry
        lax.fori_loop(0, length // CH, depth_back, 0)

        rows = [jnp.sum(gd[t], axis=0, keepdims=True) for t in range(taps)]
        rows.append(jnp.sum(gn[AUG + SLOT:AUG + 2 * SLOT, :], axis=0, keepdims=True))
        rows.append(jnp.sum(gn[AUG:AUG + SLOT, :], axis=0, keepdims=True))
        rows.append(jnp.zeros((LANES - len(rows), model), f32))
        pf = jnp.concatenate(rows, axis=0).T
        slot = 0
        drain(slot)
        nr = plan.rows_small
        for s in range(plan.shards):
            parts = [gk[s * ns:(s + 1) * ns]] + [
                pf[(2 * s + j) * ns:(2 * s + j + 1) * ns] for j in range(2)
            ]
            piece = jnp.concatenate(parts, axis=1)
            if nr > ns:
                piece = jnp.concatenate([piece, jnp.zeros((nr - ns, WIDTH), f32)], axis=0)
            stage[slot, s * nr:(s + 1) * nr, :] = piece.astype(bf16)
        outgoing("small", slot).start()
        send[slot] = "small"
        for slot in sorted(send):
            drain(slot)

    pl.run_scoped(
        back_scope,
        pltpu.VMEM((cols_m, length + 2 * PADR, LANES), f32),
        pltpu.VMEM((heads, hs + AUG, length), bf16),
        pltpu.VMEM((length, length), bf16),
        pltpu.VMEM((length, 4 * att), bf16),
        pltpu.VMEM((length, att), bf16),
        pltpu.VMEM((length, LANES), bf16),
        pltpu.VMEM((cols_a, length + 2 * PADR, LANES), f32),
        pltpu.VMEM((CV, span), bf16),
        pltpu.VMEM((taps, SLOT, model), f32),
    )


def run_mega(plan, heads, taps, hidden, cotangent, segr, gath):
    length, model = hidden.shape
    att = WIDTH
    hs = att // heads
    cols_m, cols_a = model // LANES, att // LANES
    names = [n for n in plan.offset if n != "small"]
    sh = plan.shards
    big = sh * max(plan.rows_in, plan.rows_ff)

    def body(hid, cot, sg, ga, o, h, gr, ph, *rest):
        nw = len(names)
        wts = dict(zip(names, rest[:nw]))
        mega(plan, heads, taps, length, model, hid, cot, sg, ga, o, h, gr, ph, wts, *rest[nw:])

    vm = pl.BlockSpec(memory_space=pltpu.VMEM)
    an = pl.BlockSpec(memory_space=pl.ANY)
    return pl.pallas_call(
        body,
        out_shape=(
            jax.ShapeDtypeStruct((length, model), bf16),
            jax.ShapeDtypeStruct((length, model), f32),
            jax.ShapeDtypeStruct((sh, plan.rows, WIDTH), bf16),
            jax.ShapeDtypeStruct((heads, length, length), bf16),
        ),
        in_specs=[vm, vm, vm, an],
        out_specs=(vm, vm, an, an),
        scratch_shapes=[pltpu.VMEM((sh, plan.count[n], WIDTH), bf16) for n in names]
        + [
            pltpu.VMEM((sh, plan.rows_small, WIDTH), bf16),
            pltpu.VMEM((length + 16, LANES), f32),
            pltpu.VMEM((length, LANES), f32),
            pltpu.VMEM((heads, hs + AUG, length), bf16),
            pltpu.VMEM((heads, hs + AUG, length), bf16),
            pltpu.VMEM((heads, hs + AUG, length), bf16),
            pltpu.VMEM((length, att), bf16),
            pltpu.VMEM((cols_a, length + 16, LANES), f32),
            pltpu.VMEM((length, LANES), f32),
            pltpu.VMEM((length, model), bf16),
            pltpu.VMEM((length, att), f32),
            pltpu.VMEM((length, att), bf16),
            pltpu.VMEM((length, 2 * att), bf16),
            pltpu.VMEM((att, length), f32),
            pltpu.VMEM((SLOT, length), f32),
            pltpu.VMEM((2, length, length), bf16),
            pltpu.VMEM((2 * LANES, cols_a * taps * LANES), bf16),
            pltpu.VMEM((AUG + 2 * SLOT, model), f32),
            pltpu.VMEM((length, model), bf16),
            pltpu.VMEM((2, big, WIDTH), bf16),
            pltpu.SemaphoreType.DMA((len(plan.offset) + 4,)),
        ],
        compiler_params=pltpu.CompilerParams(vmem_limit_bytes=67043328),
    )(hidden, cotangent, segr, gath)


def pack(plan, taps, w_query, w_key, w_value, w_depth, w_keyconv, w_kernel, w_convout, w_output, gain_attn, w_inter, w_outer, gain_ffn):
    ns = plan.n_small
    heads = w_kernel.shape[0] // taps
    wk = w_kernel.reshape(heads, taps, ns).transpose(2, 1, 0)
    wk = jnp.pad(wk, ((0, 0), (0, 0), (0, SLOT - heads))).reshape(ns, taps * SLOT)
    wk = jnp.pad(wk, ((0, 0), (0, LANES - taps * SLOT)))
    pf = jnp.concatenate([w_depth, gain_attn[None], gain_ffn[None]], axis=0).T
    pf = jnp.pad(pf, ((0, 0), (0, LANES - pf.shape[1])))
    small = jnp.concatenate([wk, pf[:ns], pf[ns:]], axis=1)
    small = jnp.pad(small, ((0, plan.rows_small - ns), (0, 0)))
    groups = w_inter.shape[0]
    parts = [w_query, w_key, w_value, w_keyconv, w_convout, small]
    parts += [w_output[:, j * WIDTH:(j + 1) * WIDTH] for j in range(groups)]
    parts += [w_inter[g].T for g in range(groups)]
    parts += [w_outer[g] for g in range(groups)]
    return jnp.concatenate(parts, axis=0)


def unpack(plan, taps, heads, groups, total):
    def part(name):
        return total[plan.offset[name]:plan.offset[name] + plan.count[name]]
    ns = plan.n_small
    small = part("small")[:ns]
    gk = small[:, :taps * SLOT].reshape(ns, taps, SLOT)[:, :, :heads].transpose(2, 1, 0).reshape(heads * taps, ns)
    pf = jnp.concatenate([small[:, LANES:2 * LANES], small[:, 2 * LANES:]], axis=0)
    return (
        part("query"), part("key"), part("value"),
        pf[:, :taps].T,
        part("keyconv"), gk, part("convout"),
        jnp.concatenate([part("out%d" % j) for j in range(groups)], axis=1),
        pf[:, taps],
        jnp.stack([part("inter%d" % g).T for g in range(groups)]),
        jnp.stack([part("outer%d" % g) for g in range(groups)]),
        pf[:, taps + 1],
    )


def local(hidden, segment_ids, cotangent, *weights):
    w_query, w_depth, w_kernel, w_inter, w_outer = weights[0], weights[3], weights[5], weights[9], weights[10]
    shards = lax.axis_size("shard")
    taps = w_depth.shape[0]
    heads = w_kernel.shape[0] // taps
    groups = w_inter.shape[0]
    model = hidden.shape[1]
    plan = Plan(shards, model, w_query.shape[1], w_outer.shape[1] * shards, groups)
    packed = pack(plan, taps, *weights)
    gathered = lax.all_gather(packed, "shard", axis=0)
    output, hidden_grad, grads, _ = run_mega(plan, heads, taps, hidden, cotangent, segment_ids, gathered)
    total = lax.psum_scatter(grads.reshape(shards * plan.rows, WIDTH), "shard", scatter_dimension=0, tiled=True)
    total = lax.psum(total.astype(f32), "rep")
    return (output, hidden_grad, *unpack(plan, taps, heads, groups, total))


def solution(mesh):
    both = P(("rep", "shard"), None)
    rows = P("shard", None)
    cols = P(None, "shard")
    params = (
        rows, rows, rows, cols, rows, cols, rows, rows, P("shard"),
        P(None, None, "shard"), P(None, "shard", None), P("shard"),
    )
    return jax.shard_map(
        local, mesh=mesh, in_specs=(both, both, both) + params, out_specs=(both, both) + params, check_vma=False
    )
```

time: 932 us -> 427 us (0.46)
  matrix products: 201 us -> 0 us
  other arithmetic: 127 us -> 3.21 us
  Pallas kernels: 0 us -> 122 us
  local copies, waits for them, and re-layouts: 124 us -> 18.9 us
  waiting for transfers between devices: 286 us -> 187 us
  blocking collectives: 164 us -> 80.1 us
    dot_general x47 -> x0, matrix products: 201 us -> none  [the longest x7 33.8 us: product_nt(): lax.dot_general(left, right, (((1,), (1,)), ((), ())), preferred_element_...]
    reduce_scatter x5 -> x0, waiting for transfers between devices: 198 us -> none  [the longest x1 55.9 us: local(): lax.psum_scatter(gradients[10], 'shard', scatter_dimension=1, tiled=True)]
    pallas_call x0 -> x1, Pallas kernels: none -> 122 us  [run_mega(): pl.pallas_call(body, out_shape=(jax.ShapeDtypeStruct((length, model), bf1...]
    all_gather x7 -> x0, blocking collectives: 115 us -> none  [the longest x1 19.3 us: local(): lax.all_gather(w_query, 'shard', axis=0, tiled=True)]
    all_gather x3 -> x1, waiting for transfers between devices: 0.04 us -> 91.1 us  [local(): gathered = lax.all_gather(packed, 'shard', axis=0)]
    unnamed x19 -> x3, waiting for transfers between devices: 28.4 us -> 95.5 us
    psum x1, blocking collectives: 18.1 us -> 80.1 us  [local(): total = lax.psum(total.astype(f32), 'rep')]
    psum x1 -> x0, waiting for transfers between devices: 59.6 us -> none  [local(): lax.psum((grouped[0], grouped[1], grouped[2], grouped[3], grouped[4], gro...]
  transfers between devices with their start and end apart: 14 -> 2, of which waited for: 7 -> 2; matrix products, arithmetic and copies ran while one was open for 29% -> 0% of each run, Pallas kernels for 0% -> 0%
where the time goes in v1:
time: 427 us; the launch traced here: 425 us
  waiting for transfers between devices  187 us (44%)
  Pallas kernels  122 us (29%)
  blocking collectives  80.1 us (19%)
  local copies, waits for them, and re-layouts  18.9 us (4%)
  between operations  14.3 us (3%)
    pallas_call x1, Pallas kernels, run_mega(): pl.pallas_call(body, out_shape=(jax.ShapeDtypeStruct((length, model), bf1...  122 us
    unnamed x3, waiting for transfers between devices  95.5 us
    all_gather x1, waiting for transfers between devices, local(): gathered = lax.all_gather(packed, 'shard', axis=0)  91.1 us
    psum x1, blocking collectives, local(): total = lax.psum(total.astype(f32), 'rep')  80.1 us
    unnamed x45, local copies, waits for them, and re-layouts  15.8 us
  transfers between devices with their start and end apart: 2, of which 2 were waited for; matrix products, arithmetic and copies ran while one was open for 0% of the time, Pallas kernels for 0%

profile of v1, /device:TPU:0, one launch (start us, length us, event | category | flops | bytes accessed | tf_op | source)
XLA Modules:
  0.0 425.0 jit_solution(4190104337460933354)
XLA Ops:
  7.2 0.0 copy-start.10
  7.2 0.0 copy-start.8
  7.2 0.0 copy-start.9
  7.2 0.0 all-gather.3.cloned.1.call-start
  7.3 0.9 copy.66
  8.2 0.1 copy.85
  8.3 0.7 maximum_bitcast_fusion.1
  9.0 0.1 pad_slice_fusion.1
  9.1 0.1 copy.69
  9.2 0.1 copy.70
  9.3 0.9 constant_dynamic-update-slice_fusion.4
  10.2 0.9 constant_dynamic-update-slice_fusion.3
  11.1 0.9 constant_dynamic-update-slice_fusion.2
  12.0 0.9 constant_dynamic-update-slice_fusion.1
  12.9 0.9 constant_dynamic-update-slice_fusion
  13.8 0.0 copy-done.10
  13.9 0.0 copy-done.8
  13.9 0.0 copy-done.9
  14.0 0.0 copy-start
  14.0 1.0 copy-done
  15.0 0.0 all-gather.3.cloned.1.call-update
  15.0 0.0 reduce-scatter.4.cloned.1.call-start
  15.1 91.1 %all-gather.3.cloned.1.call-done = bf16[11904,384]{1,0:T(8,128)(2,1)} async-done(((bf16[1488,384]{1,0:T(8,128)(2,1)}), bf16[11904,384]{1,0:T(8,128)(2,1)}) %all-gather.3.cloned.1.call-update) | async-done | bytes 9142288 | tf_op jit(solution)/shard_map/all_gather | solution.py:639
  106.2 121.8 %shard_map.254 = (bf16[1024,768]{1,0:T(8,128)(2,1)}, f32[1024,768]{1,0:T(8,128)}, bf16[8,1488,384]{2,1,0:T(8,128)(2,1)}, bf16[6,1024,1024]{2,1,0:T(8,128)(2,1)}) custom-call(bf16[1024,768]{1,0:T(8,128)(2,1)} %hid.1, bf16[1024,768]{1,0:T(8,128)(2,1)} %cot.1, s32[1,1024]{1,0:T(1,128)} %sg.1, bf16[8,1488,384]{2,1,0:T(8,128)(2,1)} %bitcast.44), custom_call_target="tpu_custom_call" | custom-call | tf_op jit(solution)/shard_map/pallas_call | solution.py:555
  228.0 0.0 reduce-scatter.4.cloned.1.call-update
  228.0 95.5 %reduce-scatter.4.cloned.1.call-done = bf16[1488,384]{1,0:T(8,128)(2,1)} async-done(((bf16[11904,384]{1,0:T(8,128)(2,1)}), bf16[1488,384]{1,0:T(8,128)(2,1)}) %reduce-scatter.4.cloned.1.call-update) | async-done | bytes 1142800
  323.5 1.6 copy.83
  325.1 80.1 %all-reduce.4 = f32[1488,384]{0,1:T(8,128)S(1)} all-reduce(bf16[1488,384]{0,1:T(8,128)(2,1)S(1)} %copy.83), channel_id=1, replica_groups=mesh['rep'=4,'shard'=8] {'rep'}, use_global_device_ids=true, to_apply=%region_1.2 | all-reduce | flops 571392 | bytes 3428352 | tf_op jit(solution)/shard_map/psum | solution.py:642
  405.2 0.1 slice_bitcast_fusion.5
  405.3 0.1 fusion.6
  405.4 0.6 fusion.4
  406.0 0.7 maximum_bitcast_fusion
  406.7 1.4 fusion.5
  408.0 1.2 slice_bitcast_fusion.1
  409.2 0.7 copy.77
  409.9 0.0 copy-start.6
  409.9 0.0 copy-start.7
  409.9 1.1 pad_maximum_fusion.1
  411.0 0.0 copy-start.5
  411.0 1.1 copy.81
  412.1 0.0 copy-start.4
  412.1 0.0 copy-start.3
  412.1 0.0 copy-done.6
  412.1 0.0 copy-done.7
  412.1 0.0 copy-start.2
  412.2 0.0 copy-start.1
  412.2 0.9 copy.79
  413.1 0.0 copy-done.5
  413.1 0.8 copy.78
  413.8 0.0 copy-done.4
  413.8 0.8 copy.76
  414.6 0.0 copy-done.3
  414.6 0.8 copy.75
  415.4 0.0 copy-done.2
  415.4 0.8 copy.74
  416.2 0.0 copy-done.1
  416.2 0.8 copy.73
  417.0 0.1 pad_maximum_fusion
  417.1 1.1 copy.80
  (14 shorter events, 0.2 us)
Async XLA Ops:
  7.2 6.6 %copy-start.10 = (bf16[96,768]{1,0:T(8,128)(2,1)S(1)}, bf16[96,768]{1,0:T(8,128)(2,1)}, u32[]{:S(2)}) copy-start(bf16[96,768]{1,0:T(8,128)(2,1)} %param.25) | copy-start | bytes 442372
  7.2 6.7 %copy-start.8 = (bf16[2,384,192]{1,2,0:T(8,128)(2,1)S(1)}, bf16[2,384,192]{1,2,0:T(8,128)(2,1)}, u32[]{:S(2)}) copy-start(bf16[2,384,192]{1,2,0:T(8,128)(2,1)} %param.27) | copy-start | bytes 884740
  7.2 6.7 %copy-start.9 = (bf16[2,192,384]{2,1,0:T(8,128)(2,1)S(1)}, bf16[2,192,384]{2,1,0:T(8,128)(2,1)}, u32[]{:S(2)}) copy-start(bf16[2,192,384]{2,1,0:T(8,128)(2,1)} %param.28) | copy-start | bytes 884740
  7.2 99.0 %all-gather.3.cloned.1.call-start = ((), (), s32[]{:S(2)}) async-start(), calls=%async_computation.1 | async-start | bytes 10285056 | tf_op jit(solution)/shard_map/all_gather | solution.py:639
  14.0 1.0 copy-start
  15.0 308.5 %reduce-scatter.4.cloned.1.call-start = ((), (), s32[]{:S(2)}) async-start(), calls=%async_computation.2 | async-start | bytes 10285056
  409.9 2.2 copy-start.6
  409.9 2.2 copy-start.7
  411.0 2.0 copy-start.5
  412.1 1.7 copy-start.4
  412.1 2.5 copy-start.3
  412.1 3.3 copy-start.2
  412.2 4.0 copy-start.1
Sparse Core Ops, SparseCore 0:
  15.2 90.9 all-gather.2
  228.1 95.3 reduce-scatter.3

commit v2 on v1

--- a/solution.py
+++ b/solution.py
@@ -32,26 +32,31 @@
 
 
 class Plan:
-    def __init__(self, shards, model, att, ff_rows, groups):
+    def __init__(self, reps, shards, model, att, ff_rows, groups):
+        self.reps = reps
         self.shards = shards
         self.rows_in = model // shards
         self.rows_ff = ff_rows // shards
-        self.rows_small = up(att // shards, 16)
         self.n_small = att // shards
+        self.rows_small = up(self.n_small, 16)
         self.offset = {}
         self.count = {}
-        at = 0
-        for name, n in (
-            [(k, self.rows_in) for k in ("query", "key", "value", "keyconv", "convout")]
-            + [("small", self.rows_small)]
-            + [("out0", self.rows_in), ("out1", self.rows_in)]
-            + [("inter%d" % g, self.rows_ff) for g in range(groups)]
-            + [("outer%d" % g, self.rows_ff) for g in range(groups)]
-        ):
-            self.offset[name] = at
-            self.count[name] = n
-            at += n
-        self.rows = at
+        self.chunks = []
+        self.rows = 0
+        front = [(k, self.rows_in) for k in ("query", "key", "value", "keyconv", "convout")]
+        front += [("small", self.rows_small)]
+        rest = [("out%d" % j, self.rows_in) for j in range(groups)]
+        rest += [("inter%d" % g, self.rows_ff) for g in range(groups)]
+        rest += [("outer%d" % g, self.rows_ff) for g in range(groups)]
+        for part in (front, rest):
+            at = self.rows
+            for name, n in part:
+                self.offset[name] = at
+                self.count[name] = n
+                at += n
+            chunk = up(-(-(at - self.rows) // reps), 16)
+            self.chunks.append(chunk)
+            self.rows += reps * chunk
 
 
 FRONT = ("query", "key", "value", "keyconv", "convout", "small")
@@ -601,45 +606,558 @@
     small = jnp.concatenate([wk, pf[:ns], pf[ns:]], axis=1)
     small = jnp.pad(small, ((0, plan.rows_small - ns), (0, 0)))
     groups = w_inter.shape[0]
-    parts = [w_query, w_key, w_value, w_keyconv, w_convout, small]
-    parts += [w_output[:, j * WIDTH:(j + 1) * WIDTH] for j in range(groups)]
-    parts += [w_inter[g].T for g in range(groups)]
-    parts += [w_outer[g] for g in range(groups)]
+    values = dict(query=w_query, key=w_key, value=w_value, keyconv=w_keyconv, convout=w_convout, small=small)
+    for g in range(groups):
+        values["out%d" % g] = w_output[:, g * WIDTH:(g + 1) * WIDTH]
+        values["inter%d" % g] = w_inter[g].T
+        values["outer%d" % g] = w_outer[g]
+    parts = []
+    at = 0
+    for name, start in plan.offset.items():
+        if start > at:
+            parts.append(jnp.zeros((start - at, WIDTH), bf16))
+        parts.append(values[name])
+        at = start + plan.count[name]
+    if plan.rows > at:
+        parts.append(jnp.zeros((plan.rows - at, WIDTH), bf16))
     return jnp.concatenate(parts, axis=0)
 
 
 def unpack(plan, taps, heads, groups, total):
-    def part(name):
-        return total[plan.offset[name]:plan.offset[name] + plan.count[name]]
-    ns = plan.n_small
-    small = part("small")[:ns]
-    gk = small[:, :taps * SLOT].reshape(ns, taps, SLOT)[:, :, :heads].transpose(2, 1, 0).reshape(heads * taps, ns)
-    pf = jnp.concatenate([small[:, LANES:2 * LANES], small[:, 2 * LANES:]], axis=0)
-    return (
-        part("query"), part("key"), part("value"),
-        pf[:, :taps].T,
-        part("keyconv"), gk, part("convout"),
-        jnp.concatenate([part("out%d" % j) for j in range(groups)], axis=1),
-        pf[:, taps],
-        jnp.stack([part("inter%d" % g).T for g in range(groups)]),
-        jnp.stack([part("outer%d" % g) for g in range(groups)]),
-        pf[:, taps + 1],
+    ns, rin, rff = plan.n_small, plan.rows_in, plan.rows_ff
+    model = rin * plan.shards
+
+    def body(src, gq, gkey, gv, gd, gkc, gker, gco, gout, gga, gin, gou, ggf):
+        def part(name):
+            return src[plan.offset[name]:plan.offset[name] + plan.count[name], :].astype(f32)
+        for name, ref in (("query", gq), ("key", gkey), ("value", gv), ("keyconv", gkc), ("convout", gco)):
+            ref[...] = part(name)
+        for j in range(groups):
+            gout[:, j * WIDTH:(j + 1) * WIDTH] = part("out%d" % j)
+            gin[j] = part("inter%d" % j).T
+            gou[j] = part("outer%d" % j)
+        small = part("small")[:ns]
+        turned = small[:, 0:LANES].T
+        for h in range(heads):
+            for t in range(taps):
+                gker[h * taps + t:h * taps + t + 1, :] = turned[t * SLOT + h:t * SLOT + h + 1]
+        pf = jnp.concatenate([small[:, LANES:2 * LANES], small[:, 2 * LANES:]], axis=0).T
+        gd[...] = pf[0:taps]
+        gga[...] = pf[taps:taps + 1]
+        ggf[...] = pf[taps + 1:taps + 2]
+
+    def out(*dims):
+        return jax.ShapeDtypeStruct(dims, f32)
+    square = out(rin, WIDTH)
+    parts = list(pl.pallas_call(
+        body,
+        out_shape=(
+            square, square, square, out(taps, rin), square, out(heads * taps, ns), square, out(rin, model),
+            out(1, rin), out(groups, WIDTH, rff), out(groups, rff, WIDTH), out(1, rin),
+        ),
+    )(total))
+    for i in (8, 11):
+        parts[i] = parts[i].reshape(rin)
+    return tuple(parts)
+
+
+class Place:
+    def __init__(self, reps, shards):
+        side = math.isqrt(reps)
+        self.sy, self.sx = (side, side) if side * side == reps else (1, reps)
+        self.cores = 2 if shards % 2 == 0 else 1
+        self.nz = shards // self.cores
+        self.reps = reps
+        self.shard = lax.axis_index("shard")
+        self.rep = lax.axis_index("rep")
+        self.z = self.shard // self.cores
+        self.core = self.shard % self.cores
+        self.py = self.rep // self.sx
+        self.px = self.rep % self.sx
+
+    def at_x(self, d):
+        return lax.rem(self.px + d, self.sx)
+
+    def at_y(self, d):
+        return lax.rem(self.py + d, self.sy)
+
+    def id(self, rep=None, shard=None):
+        return {
+            "rep": self.rep if rep is None else rep,
+            "shard": self.shard if shard is None else shard,
+        }
+
+    def xpeer(self, d):
+        return self.id(rep=self.py * self.sx + self.at_x(d))
+
+    def ypeer(self, d):
+        return self.id(rep=self.at_y(d) * self.sx + self.px)
+
+    def partner(self):
+        return self.id(shard=self.z * self.cores + (1 - self.core))
+
+    def right(self):
+        return self.id(shard=self.shard + self.cores)
+
+    def left(self):
+        return self.id(shard=self.shard - self.cores)
+
+    def barrier(self):
+        sem = pltpu.get_barrier_semaphore()
+
+        def hello(device):
+            pl.semaphore_signal(sem, inc=1, device_id=device, device_id_type=pl.DeviceIdType.MESH)
+
+        for d in range(1, self.sx):
+            hello(self.xpeer(d))
+        for d in range(1, self.sy):
+            hello(self.ypeer(d))
+        if self.cores == 2:
+            hello(self.partner())
+        pl.when(self.z > 0)(lambda: hello(self.left()))
+        pl.when(self.z < self.nz - 1)(lambda: hello(self.right()))
+        steady = self.sx + self.sy - 2 + self.cores - 1
+        ends = jnp.where(self.z > 0, 1, 0) + jnp.where(self.z < self.nz - 1, 1, 0)
+        pl.semaphore_wait(sem, steady + ends)
+
+
+def remote(src, dst, send, recv, device):
+    return pltpu.make_async_remote_copy(
+        src_ref=src, dst_ref=dst, send_sem=send, recv_sem=recv,
+        device_id=device, device_id_type=pl.DeviceIdType.MESH,
     )
+
+
+class Gather:
+    def __init__(self, place, base, chunk, own, full, sems):
+        self.p, self.base, self.chunk, self.own, self.full = place, base, chunk, own, full
+        self.item, self.zsend, self.share = sems
+        self.ha = up(chunk // 2, 16)
+
+    @staticmethod
+    def sems(place_dims):
+        reps, nz = place_dims
+        return [
+            pltpu.SemaphoreType.DMA((nz, reps, 2)),
+            pltpu.SemaphoreType.DMA((2, nz)),
+            pltpu.SemaphoreType.DMA((4,)),
+        ]
+
+    def rows(self, q, half=None):
+        start = self.base + q * self.chunk
+        if half is None:
+            return pl.ds(pl.multiple_of(start, 16), self.chunk)
+        if half == 0:
+            return pl.ds(pl.multiple_of(start, 16), self.ha)
+        return pl.ds(pl.multiple_of(start + self.ha, 16), self.chunk - self.ha)
+
+    def move(self, zs, q, half, send, recv, device, src=None):
+        at = self.full.at[zs * self.p.cores + self.p.core, self.rows(q, half)]
+        return remote(at if src is None else src, at, send, recv, device)
+
+    def plane(self, zs, q, half, device, which):
+        self.move(zs, q, half, self.share.at[0], self.item.at[zs, q, which], device).start()
+
+    def hand(self, zs, q):
+        if self.p.cores == 2:
+            self.move(zs, q, None, self.share.at[1], self.share.at[2], self.p.partner()).start()
+
+    def arrived(self, zs, q, half, which):
+        self.move(zs, q, half, self.share.at[0], self.item.at[zs, q, which], self.p.partner()).wait_recv()
+
+    def start(self):
+        p = self.p
+        mine = self.own.at[self.rows(p.rep)]
+        pl.when(p.z < p.nz - 1)(lambda: self.move(
+            p.z, p.rep, None, self.zsend.at[0, 0], self.item.at[p.z, p.rep, 0], p.right(), mine).start())
+        pl.when(p.z > 0)(lambda: self.move(
+            p.z, p.rep, None, self.zsend.at[1, 0], self.item.at[p.z, p.rep, 0], p.left(), mine).start())
+        if p.cores == 2:
+            self.whole(p.partner()).start()
+        self.keep().start()
+
+    def whole(self, device):
+        r = pl.ds(self.base, self.p.reps * self.chunk)
+        return remote(self.own.at[r], self.full.at[self.p.shard, r], self.share.at[1], self.share.at[2], device)
+
+    def keep(self):
+        r = pl.ds(self.base, self.p.reps * self.chunk)
+        return pltpu.make_async_copy(self.own.at[r], self.full.at[self.p.shard, r], self.share.at[3])
+
+    def both(self, k, body):
+        p = self.p
+        pl.when(p.z - k >= 0)(lambda: body(p.z - k, 0))
+        pl.when(p.z + k < p.nz)(lambda: body(p.z + k, 1))
+
+    def along(self, k):
+        p = self.p
+
+        def body(zs, way):
+            self.arrived(zs, p.rep, None, 0)
+            more = p.z < p.nz - 1 if way == 0 else p.z > 0
+            pl.when(more)(lambda: self.move(
+                zs, p.rep, None, self.zsend.at[way, k], self.item.at[zs, p.rep, 0],
+                p.right() if way == 0 else p.left()).start())
+            for d in range(1, p.sx):
+                self.plane(zs, p.rep, None, p.xpeer(d), 0)
+            for d in range(1, p.sy):
+                self.plane(zs, p.rep, None, p.ypeer(d), 0)
+            self.hand(zs, p.rep)
+        self.both(k, body)
+
+    def across(self, k):
+        p = self.p
+
+        def body(zs, way):
+            for d in range(1, p.sx):
+                q = p.py * p.sx + p.at_x(d)
+                self.arrived(zs, q, None, 0)
+                for e in range(1, p.sy):
+                    self.plane(zs, q, 0, p.ypeer(e), 0)
+                self.hand(zs, q)
+            for d in range(1, p.sy):
+                q = p.at_y(d) * p.sx + p.px
+                self.arrived(zs, q, None, 0)
+                for e in range(1, p.sx):
+                    self.plane(zs, q, 1, p.xpeer(e), 1)
+                self.hand(zs, q)
+        self.both(k, body)
+
+    def corner(self, k):
+        p = self.p
+
+        def body(zs, way):
+            for d in range(1, p.sy):
+                for e in range(1, p.sx):
+                    q = p.at_y(d) * p.sx + p.at_x(e)
+                    self.arrived(zs, q, 0, 0)
+                    self.arrived(zs, q, 1, 1)
+                    self.hand(zs, q)
+        self.both(k, body)
+
+    def finish(self):
+        p = self.p
+        self.keep().wait()
+        if p.cores == 2:
+            r = self.full.at[pl.ds(0, p.nz), pl.ds(self.base, p.reps * self.chunk)]
+            both = remote(r, r, self.share.at[1], self.share.at[2], p.partner())
+            both.wait_recv()
+            both.wait_send()
+        if p.nz > 1 and p.reps > 1:
+            r = self.full.at[pl.ds(0, p.nz - 1), pl.ds(0, (p.reps - 1) * self.chunk)]
+            remote(r, r, self.share.at[0], self.share.at[2], p.partner()).wait_send()
+        for way in range(2):
+            for k in range(p.nz - 1):
+                if way == 0:
+                    sent = (p.z - k >= 0) & (p.z < p.nz - 1)
+                else:
+                    sent = (p.z + k < p.nz) & (p.z > 0)
+                pl.when(sent)(lambda way=way, k=k: self.move(
+                    p.z, p.rep, None, self.zsend.at[way, k], self.share.at[2], p.partner()).wait_send())
+
+
+def chunk_of(rows, reps):
+    return up(-(-rows // reps), 16)
+
+
+class Reduce:
+    def __init__(self, place, chunk, src, land, bufs, done, sems):
+        self.p, self.chunk, self.src, self.land, self.done = place, chunk, src, land, done
+        self.xa, self.yb, self.ya, self.xb, self.zr, self.zl = bufs
+        self.near, self.sx, self.sy, self.s2x, self.s2y, self.zin, self.fin, self.out = sems
+        self.ha = up(chunk // 2, 16)
+        p = place
+        self.order = []
+        lo, hi = 0, p.nz - 1
+        while lo <= hi:
+            self.order.append(hi)
+            if lo < hi:
+                self.order.append(lo)
+            lo, hi = lo + 1, hi - 1
+
+    @staticmethod
+    def buffers(reps, shards, chunk):
+        side = math.isqrt(reps)
+        sy, sx = (side, side) if side * side == reps else (1, reps)
+        nz = shards // (2 if shards % 2 == 0 else 1)
+        ha = up(chunk // 2, 16)
+        hb = chunk - ha
+        dx, dy = max(sx - 1, 1), max(sy - 1, 1)
+        return [
+            pltpu.VMEM((dx, nz, sy, ha, WIDTH), bf16),
+            pltpu.VMEM((dy, nz, sx, hb, WIDTH), bf16),
+            pltpu.VMEM((dy, nz, ha, WIDTH), bf16),
+            pltpu.VMEM((dx, nz, hb, WIDTH), bf16),
+            pltpu.VMEM((nz, chunk, WIDTH), bf16),
+            pltpu.VMEM((nz, chunk, WIDTH), bf16),
+        ]
+
+    @staticmethod
+    def sems(reps, shards):
+        side = math.isqrt(reps)
+        sy, sx = (side, side) if side * side == reps else (1, reps)
+        nz = shards // (2 if shards % 2 == 0 else 1)
+        dx, dy = max(sx - 1, 1), max(sy - 1, 1)
+        dma = pltpu.SemaphoreType.DMA
+        return [
+            dma((nz,)), dma((dx, nz)), dma((dy, nz)), dma((dx, nz)), dma((dy, nz)),
+            dma((2, nz)), dma((sy, sx, 2)), dma((7,)),
+        ]
+
+    def rows(self, q, half=None):
+        start = q * self.chunk
+        if half is None:
+            return pl.ds(pl.multiple_of(start, 16), self.chunk)
+        if half == 0:
+            return pl.ds(pl.multiple_of(start, 16), self.ha)
+        return pl.ds(pl.multiple_of(start + self.ha, 16), self.chunk - self.ha)
+
+    def to_partner(self, zd, device):
+        other = zd * self.p.cores + (1 - self.p.core)
+        return remote(self.src(other), self.land.at[zd], self.out.at[0], self.near.at[zd], device)
+
+    def start(self):
+        for zd in self.order:
+            self.to_partner(zd, self.p.partner()).start()
+
+    def tiles(self, body, n):
+        step = 16
+        def one(i, carry):
+            body(pl.multiple_of(i * step, step), step)
+            return carry
+        lax.fori_loop(0, n // step, one, 0)
+
+    def add_into(self, ref, start, n, others):
+        def body(i, step):
+            r = pl.ds(pl.multiple_of(start + i, 16), step)
+            total = ref[r, :].astype(f32)
+            for other in others:
+                total = total + other[pl.ds(i, step), :].astype(f32)
+            ref[r, :] = total.astype(bf16)
+        self.tiles(body, n)
+
+    def cores(self, zd, own):
+        p = self.p
+        self.to_partner(zd, p.partner()).wait_recv()
+        self.add_into(self.land.at[zd], 0, p.reps * self.chunk, [own(zd)])
+        for d in range(1, p.sx):
+            for y in range(p.sy):
+                remote(
+                    self.land.at[zd, self.rows(y * p.sx + p.at_x(d), 0)],
+                    self.xa.at[p.sx - d - 1, zd, y],
+                    self.out.at[1], self.sx.at[p.sx - d - 1, zd], p.xpeer(d),
+                ).start()
+        for d in range(1, p.sy):
+            for x in range(p.sx):
+                remote(
+                    self.land.at[zd, self.rows(p.at_y(d) * p.sx + x, 1)],
+                    self.yb.at[p.sy - d - 1, zd, x],
+                    self.out.at[2], self.sy.at[p.sy - d - 1, zd], p.ypeer(d),
+                ).start()
+
+    def first(self, zd):
+        p = self.p
+        here = self.land.at[zd]
+        for d in range(p.sx - 1):
+            remote(self.xa.at[d, zd], self.xa.at[d, zd], self.out.at[1], self.sx.at[d, zd], p.partner()).wait_recv()
+        for d in range(p.sy - 1):
+            remote(self.yb.at[d, zd], self.yb.at[d, zd], self.out.at[2], self.sy.at[d, zd], p.partner()).wait_recv()
+        for y in range(p.sy):
+            if p.sx > 1:
+                self.add_into(here, (y * p.sx + p.px) * self.chunk, self.ha, [self.xa.at[d, zd, y] for d in range(p.sx - 1)])
+        for x in range(p.sx):
+            if p.sy > 1:
+                self.add_into(here, (p.py * p.sx + x) * self.chunk + self.ha, self.chunk - self.ha, [self.yb.at[d, zd, x] for d in range(p.sy - 1)])
+        for d in range(1, p.sy):
+            remote(
+                self.land.at[zd, self.rows(p.at_y(d) * p.sx + p.px, 0)],
+                self.ya.at[p.sy - d - 1, zd],
+                self.out.at[3], self.s2y.at[p.sy - d - 1, zd], p.ypeer(d),
+            ).start()
+        for d in range(1, p.sx):
+            remote(
+                self.land.at[zd, self.rows(p.py * p.sx + p.at_x(d), 1)],
+                self.xb.at[p.sx - d - 1, zd],
+                self.out.at[4], self.s2x.at[p.sx - d - 1, zd], p.xpeer(d),
+            ).start()
+
+    def second(self, zd):
+        p = self.p
+        here = self.land.at[zd]
+        for d in range(p.sy - 1):
+            remote(self.ya.at[d, zd], self.ya.at[d, zd], self.out.at[3], self.s2y.at[d, zd], p.partner()).wait_recv()
+        for d in range(p.sx - 1):
+            remote(self.xb.at[d, zd], self.xb.at[d, zd], self.out.at[4], self.s2x.at[d, zd], p.partner()).wait_recv()
+        if p.sy > 1:
+            self.add_into(here, p.rep * self.chunk, self.ha, [self.ya.at[d, zd] for d in range(p.sy - 1)])
+        if p.sx > 1:
+            self.add_into(here, p.rep * self.chunk + self.ha, self.chunk - self.ha, [self.xb.at[d, zd] for d in range(p.sx - 1)])
+
+    def hop(self, zd, way):
+        buf = self.zr if way == 0 else self.zl
+        return remote(
+            self.land.at[zd, self.rows(self.p.rep)], buf.at[zd], self.out.at[5], self.zin.at[way, zd],
+            self.p.right() if way == 0 else self.p.left(),
+        )
+
+    def line(self, zd):
+        p = self.p
+        here = self.land.at[zd]
+
+        def go(way, inner):
+            def more():
+                self.hop(zd, way).wait_recv()
+                self.add_into(here, p.rep * self.chunk, self.chunk, [(self.zr if way == 0 else self.zl).at[zd]])
+            pl.when(inner)(more)
+            self.hop(zd, way).start()
+        pl.when(zd > p.z)(lambda: go(0, p.z > 0))
+        pl.when(zd < p.z)(lambda: go(1, p.z < p.nz - 1))
+
+    def total(self):
+        p = self.p
+        for way, there in ((0, p.z > 0), (1, p.z < p.nz - 1)):
+            def more(way=way):
+                self.hop(p.z, way).wait_recv()
+                self.add_into(self.land.at[p.z], p.rep * self.chunk, self.chunk, [(self.zr if way == 0 else self.zl).at[p.z]])
+            pl.when(there)(more)
+
+        def copy(i, step):
+            r = pl.ds(pl.multiple_of(p.rep * self.chunk + i, 16), step)
+            self.done[r, :] = self.land[p.z, r, :]
+        self.tiles(copy, self.chunk)
+        for d in range(1, p.sx):
+            self.spread(p.rep, None, p.xpeer(d), 0, p.sx - d, 0).start()
+        for d in range(1, p.sy):
+            self.spread(p.rep, None, p.ypeer(d), p.sy - d, 0, 0).start()
+
+    def spread(self, q, half, device, dy, dx, which):
+        at = self.done.at[self.rows(q, half)]
+        return remote(at, at, self.out.at[6], self.fin.at[dy, dx, which], device)
+
+    def around(self):
+        p = self.p
+        for d in range(1, p.sx):
+            q = p.py * p.sx + p.at_x(d)
+            self.spread(q, None, p.partner(), 0, d, 0).wait_recv()
+            for e in range(1, p.sy):
+                self.spread(q, 0, p.ypeer(e), p.sy - e, d, 0).start()
+        for d in range(1, p.sy):
+            q = p.at_y(d) * p.sx + p.px
+            self.spread(q, None, p.partner(), d, 0, 0).wait_recv()
+            for e in range(1, p.sx):
+                self.spread(q, 1, p.xpeer(e), d, p.sx - e, 1).start()
+
+    def finish(self):
+        p = self.p
+        for d in range(1, p.sy):
+            for e in range(1, p.sx):
+                q = p.at_y(d) * p.sx + p.at_x(e)
+                self.spread(q, 0, p.partner(), d, e, 0).wait_recv()
+                self.spread(q, 1, p.partner(), d, e, 1).wait_recv()
+
+        def sent(ref, i):
+            remote(ref, ref, self.out.at[i], self.near.at[0], p.partner()).wait_send()
+        sent(self.land, 0)
+        if p.sx > 1:
+            sent(self.xa, 1)
+            sent(self.xb, 4)
+        if p.sy > 1:
+            sent(self.yb, 2)
+            sent(self.ya, 3)
+        if p.nz > 1:
+            sent(self.zr.at[pl.ds(0, p.nz - 1)], 5)
+        if p.reps > 1:
+            sent(self.done.at[pl.ds(0, (p.reps - 1) * self.chunk)], 6)
+
+
+def run_gather(reps, shards, own, chunks):
+    rows = own.shape[0]
+    nz = shards // (2 if shards % 2 == 0 else 1)
+
+    def body(own_ref, full, *sems):
+        place = Place(reps, shards)
+        place.barrier()
+        parts = []
+        base = 0
+        for i, chunk in enumerate(chunks):
+            parts.append(Gather(place, base, chunk, own_ref, full, sems[3 * i:3 * i + 3]))
+            base += reps * chunk
+        for g in parts:
+            g.start()
+        for g in parts:
+            for k in range(1, place.nz):
+                g.along(k)
+            for k in range(1, place.nz):
+                g.across(k)
+        for g in parts:
+            for k in range(1, place.nz):
+                g.corner(k)
+        for g in parts:
+            g.finish()
+
+    return pl.pallas_call(
+        body,
+        out_shape=jax.ShapeDtypeStruct((shards, rows, WIDTH), bf16),
+        in_specs=[pl.BlockSpec(memory_space=pltpu.VMEM)],
+        out_specs=pl.BlockSpec(memory_space=pl.ANY),
+        scratch_shapes=[s for _ in chunks for s in Gather.sems((reps, nz))],
+        compiler_params=pltpu.CompilerParams(collective_id=1, has_side_effects=True),
+    )(own)
+
+
+def run_reduce(reps, shards, grads):
+    rows = grads.shape[1]
+    chunk = rows // reps
+    cores = 2 if shards % 2 == 0 else 1
+    nz = shards // cores
+    nbuf = 6
+
+    def body(src, done, land, own, *rest):
+        place = Place(reps, shards)
+        bufs, sems, local = rest[:nbuf], rest[nbuf:-1], rest[-1]
+        red = Reduce(place, chunk, lambda s: src.at[s], land, bufs, done, sems)
+
+        def fetch(zd):
+            return pltpu.make_async_copy(src.at[zd * cores + place.core], own.at[zd], local.at[zd])
+        for zd in red.order:
+            fetch(zd).start()
+        place.barrier()
+        red.start()
+        for zd in red.order:
+            fetch(zd).wait()
+            red.cores(zd, lambda zd: own.at[zd])
+        for zd in red.order:
+            red.first(zd)
+        for zd in red.order:
+            red.second(zd)
+            red.line(zd)
+        red.total()
+        red.around()
+        red.finish()
+
+    return pl.pallas_call(
+        body,
+        out_shape=jax.ShapeDtypeStruct((rows, WIDTH), bf16),
+        in_specs=[pl.BlockSpec(memory_space=pl.ANY)],
+        out_specs=pl.BlockSpec(memory_space=pltpu.VMEM),
+        scratch_shapes=[pltpu.VMEM((nz, rows, WIDTH), bf16), pltpu.VMEM((nz, rows, WIDTH), bf16)]
+        + Reduce.buffers(reps, shards, chunk) + Reduce.sems(reps, shards) + [pltpu.SemaphoreType.DMA((nz,))],
+        compiler_params=pltpu.CompilerParams(collective_id=2, has_side_effects=True, vmem_limit_bytes=60 << 20),
+    )(grads)
 
 
 def local(hidden, segment_ids, cotangent, *weights):
     w_query, w_depth, w_kernel, w_inter, w_outer = weights[0], weights[3], weights[5], weights[9], weights[10]
-    shards = lax.axis_size("shard")
+    shards, reps = lax.axis_size("shard"), lax.axis_size("rep")
     taps = w_depth.shape[0]
     heads = w_kernel.shape[0] // taps
     groups = w_inter.shape[0]
     model = hidden.shape[1]
-    plan = Plan(shards, model, w_query.shape[1], w_outer.shape[1] * shards, groups)
+    plan = Plan(reps, shards, model, w_query.shape[1], w_outer.shape[1] * shards, groups)
     packed = pack(plan, taps, *weights)
-    gathered = lax.all_gather(packed, "shard", axis=0)
+    gathered = run_gather(reps, shards, packed, plan.chunks)
     output, hidden_grad, grads, _ = run_mega(plan, heads, taps, hidden, cotangent, segment_ids, gathered)
-    total = lax.psum_scatter(grads.reshape(shards * plan.rows, WIDTH), "shard", scatter_dimension=0, tiled=True)
-    total = lax.psum(total.astype(f32), "rep")
+    total = run_reduce(reps, shards, grads)
     return (output, hidden_grad, *unpack(plan, taps, heads, groups, total))
 
 

time: 427 us -> 264 us (0.62)
  waiting for transfers between devices: 187 us -> 0 us
  Pallas kernels: 122 us -> 250 us
  blocking collectives: 80.1 us -> 0 us
  between operations: 14.3 us -> 0.82 us
  local copies, waits for them, and re-layouts: 18.9 us -> 11.2 us
    pallas_call x0 -> x3, Pallas kernels: none -> 128 us  [the longest x1 77.6 us: run_reduce(): pl.pallas_call(body, out_shape=jax.ShapeDtypeStruct((rows, WIDTH), bf16),...]
    unnamed x3 -> x0, waiting for transfers between devices: 95.5 us -> none
    all_gather x1 -> x0, waiting for transfers between devices: 91.1 us -> none  [local(): gathered = lax.all_gather(packed, 'shard', axis=0)]
    psum x1 -> x0, blocking collectives: 80.1 us -> none  [local(): total = lax.psum(total.astype(f32), 'rep')]
    unnamed x45 -> x23, local copies, waits for them, and re-layouts: 15.8 us -> 11 us
  transfers between devices with their start and end apart: 2 -> 0, of which waited for: 2 -> 0; matrix products, arithmetic and copies ran while one was open for 0% -> 0% of each run, Pallas kernels for 0% -> 0%
where the time goes in v2:
time: 264 us; the launch traced here: 263 us
  Pallas kernels  250 us (95%)
  local copies, waits for them, and re-layouts  11.2 us (4%)
    pallas_call x1, Pallas kernels, run_mega(): pl.pallas_call(body, out_shape=(jax.ShapeDtypeStruct((length, model), bf1...  122 us
    pallas_call x1, Pallas kernels, run_reduce(): pl.pallas_call(body, out_shape=jax.ShapeDtypeStruct((rows, WIDTH), bf16),...  77.6 us
    pallas_call x1, Pallas kernels, run_gather(): pl.pallas_call(body, out_shape=jax.ShapeDtypeStruct((shards, rows, WIDTH)...  47.8 us
    unnamed x23, local copies, waits for them, and re-layouts  11 us

profile of v2, /device:TPU:0, one launch (start us, length us, event | category | flops | bytes accessed | tf_op | source)
XLA Modules:
  0.0 262.9 jit_solution(9824154518192166646)
XLA Ops:
  0.6 0.0 copy-start.2
  0.7 0.0 copy-start.1
  0.7 0.0 copy-start.3
  0.7 0.8 pad_maximum_fusion
  1.5 0.8 copy.43
  2.4 0.1 copy.45
  2.4 0.1 copy.46
  2.6 0.9 constant_dynamic-update-slice_fusion.5
  3.5 0.9 constant_dynamic-update-slice_fusion.4
  4.4 0.9 constant_dynamic-update-slice_fusion.3
  5.3 0.9 constant_dynamic-update-slice_fusion.2
  6.2 0.9 constant_dynamic-update-slice_fusion.1
  7.1 0.9 slice_dynamic-update-slice_fusion.1
  8.0 0.0 copy-done.3
  8.1 0.0 copy-done.1
  8.1 0.0 copy-done.2
  8.2 0.0 copy-start
  8.2 1.0 copy-done
  9.2 47.8 %shard_map.254.ga = bf16[8,1536,384]{2,1,0:T(8,128)(2,1)} custom-call(bf16[1536,384]{1,0:T(8,128)(2,1)} %copy-done), custom_call_target="tpu_custom_call" | custom-call | tf_op jit(solution)/shard_map/pallas_call | solution.py:1098
  57.0 121.8 %shard_map.255 = (bf16[1024,768]{1,0:T(8,128)(2,1)}, f32[1024,768]{1,0:T(8,128)}, bf16[8,1536,384]{2,1,0:T(8,128)(2,1)}, bf16[6,1024,1024]{2,1,0:T(8,128)(2,1)}) custom-call(bf16[1024,768]{1,0:T(8,128)(2,1)} %hid.1, bf16[1024,768]{1,0:T(8,128)(2,1)} %cot.1, s32[1,1024]{1,0:T(1,128)} %sg.1, bf16[8,1536,384]{2,1,0:T(8,128)(2,1)} %shard_map.254.ga), custom_call_target="tpu_custom_call" | custom-call | tf_op jit(solution)/shard_map/pallas_call | solution.py:560
  178.8 77.6 %shard_map.256.src = bf16[1536,384]{1,0:T(8,128)(2,1)} custom-call(bf16[8,1536,384]{2,1,0:T(8,128)(2,1)} %get-tuple-element.31.src), custom_call_target="tpu_custom_call" | custom-call | tf_op jit(solution)/shard_map/pallas_call | solution.py:1138
  256.4 2.8 %shard_map.257 = (f32[96,384]{1,0:T(8,128)}, f32[96,384]{1,0:T(8,128)}, f32[96,384]{1,0:T(8,128)}, f32[9,96]{1,0:T(8,128)}, f32[96,384]{1,0:T(8,128)}, /*index=5...) custom-call(bf16[1536,384]{1,0:T(8,128)(2,1)} %shard_map.256.src), custom_call_target="tpu_custom_call" | custom-call | tf_op jit(solution)/shard_map/pallas_call | solution.py:652
  259.3 1.4 copy.47
  260.7 2.2 copy.48
  (11 shorter events, 0.2 us)
Async XLA Ops:
  0.6 7.5 %copy-start.2 = (bf16[2,192,384]{2,1,0:T(8,128)(2,1)S(1)}, bf16[2,192,384]{2,1,0:T(8,128)(2,1)}, u32[]{:S(2)}) copy-start(bf16[2,192,384]{2,1,0:T(8,128)(2,1)} %param.28) | copy-start | bytes 884740
  0.7 7.4 %copy-start.1 = (bf16[2,384,192]{1,2,0:T(8,128)(2,1)S(1)}, bf16[2,384,192]{1,2,0:T(8,128)(2,1)}, u32[]{:S(2)}) copy-start(bf16[2,384,192]{1,2,0:T(8,128)(2,1)} %param.27) | copy-start | bytes 884740
  0.7 7.4 %copy-start.3 = (bf16[96,768]{1,0:T(8,128)(2,1)S(1)}, bf16[96,768]{1,0:T(8,128)(2,1)}, u32[]{:S(2)}) copy-start(bf16[96,768]{1,0:T(8,128)(2,1)} %param.25) | copy-start | bytes 442372
  8.2 1.0 copy-start
